TPU v7x, 32 devices: a whole 2x2x4 slice. The times are simulated.
32 devices in a mesh: dp: 16 (over z, x, core), tensor: 2 (over y).
Axes of the slice: x: 2, y: 2, z: 4, core: 2. Of those that a mesh axis runs over, the one named last changes fastest.
Arguments:
- tokens: bfloat16 [4096, 1024], P('dp'), may hold values from -6 to 6
- cotangent: bfloat16 [4096, 1024], P('dp'), may hold values from -6 to 6
- seq_lens: int32 [64], P('dp'), may hold values from 0 to 256, as said below
- layer_norm_gain: float32 [2, 1024], replicated, may hold values from 0.1 to 1.9
- layer_norm_bias: float32 [2, 1024], replicated, may hold values from -2 to 2
- w_qkv: bfloat16 [3, 1024, 1024], P(None, 'dp', 'tensor'), may hold values from -1 to 1
- b_qv: float32 [2, 1024], P(None, 'tensor'), may hold values from -2 to 2
- w_out: bfloat16 [1024, 1024], P('dp', 'tensor'), may hold values from -0.75 to 0.75
- b_out: float32 [1024], replicated, may hold values from -2 to 2
- w_fc1: bfloat16 [1024, 4096], P('dp', 'tensor'), may hold values from -0.1875 to 0.1875
- b_fc1: float32 [4096], P('tensor'), may hold values from -3 to 3
- w_fc2: bfloat16 [1024, 4096], P('dp', 'tensor'), may hold values from -0.09375 to 0.09375
- b_fc2: float32 [1024], replicated, may hold values from -2 to 2
Outputs:
- output: bfloat16 [4096, 1024], P('dp')
- grad_tokens: float32 [4096, 1024], P('dp')
- grad_norm_gain: float32 [2, 1024], replicated
- grad_norm_bias: float32 [2, 1024], replicated
- grad_w_qkv: float32 [3, 1024, 1024], P(None, 'dp', 'tensor')
- grad_b_qv: float32 [2, 1024], P(None, 'tensor')
- grad_w_out: float32 [1024, 1024], P('dp', 'tensor')
- grad_b_out: float32 [1024], replicated
- grad_w_fc1: float32 [1024, 4096], P('dp', 'tensor')
- grad_b_fc1: float32 [4096], P('tensor')
- grad_w_fc2: float32 [1024, 4096], P('dp', 'tensor')
- grad_b_fc2: float32 [1024], replicated
Inputs may be any that keep to these rules, and one draw needn't show every extreme that they name: `seq_lens`: each device's 4 lengths are whole sequences laid one after another from its first row; they sum to at most 256, and some device holds a single sequence of exactly 256 rows. Rows after a device's sequences are padding.
All inputs are finite; a program needn't handle non-finite values.
Results may differ from a plain program's by a relative error of at most 0.014.
Values may be sent and summed in bfloat16 or wider, within the bound.
A program may use at most 128 MiB of HBM per device.

v0:
```python
import jax
import jax.numpy as jnp
from jax import lax
from jax.sharding import PartitionSpec as P

HEAD_DIM = 64


NORM_EPS = 1e-05
GELU_COEF = 0.7978845608028654


def product(spec, left, right):
    return jnp.einsum(spec, left, right, preferred_element_type=jnp.float32)


def seq_masks(lengths, row_count):
    ends = jnp.cumsum(lengths, dtype=jnp.int32)
    places = jnp.arange(row_count, dtype=jnp.int32)
    segment = jnp.sum((places[:, None] >= ends[None, :]).astype(jnp.int32), axis=1)
    allowed = (segment[:, None] == segment[None, :]) & (places[:, None] >= places[None, :])
    live_rows = places < ends[-1]
    return (allowed, live_rows)


def layer_norm_forward(hidden, gain, shift):
    center = hidden - jnp.mean(hidden, axis=-1, keepdims=True)
    inv_std = lax.rsqrt(jnp.mean(center * center, axis=-1, keepdims=True) + NORM_EPS)
    normal_x = center * inv_std
    return (normal_x * gain + shift, normal_x, inv_std)


def layer_norm_backward(grad_out, gain, normal_x, inv_std):
    scaled = grad_out * gain
    return inv_std * (
        scaled
        - jnp.mean(scaled, axis=-1, keepdims=True)
        - normal_x * jnp.mean(scaled * normal_x, axis=-1, keepdims=True)
    )


def gelu_parts(pre_act):
    inner = GELU_COEF * (pre_act + 0.044715 * pre_act * pre_act * pre_act)
    tanh_val = jnp.tanh(inner)
    value = 0.5 * pre_act * (1.0 + tanh_val)
    slope = 0.5 * (1.0 + tanh_val) + 0.5 * pre_act * (1.0 - tanh_val * tanh_val) * GELU_COEF * (
        1.0 + 3.0 * 0.044715 * pre_act * pre_act
    )
    return (value, slope)


def split_heads(matrix):
    return matrix.reshape(matrix.shape[0], matrix.shape[1] // HEAD_DIM, HEAD_DIM)


def head_scores(query, key_rows, allowed):
    scores = product("qhd,khd->hqk", split_heads(query), split_heads(key_rows)) * HEAD_DIM ** (-0.5)
    return jnp.where(allowed[None], scores, -1e30)


def attend(query, key_rows, value, allowed):
    scores = head_scores(query, key_rows, allowed)
    row_max = jnp.max(scores, axis=-1, keepdims=True)
    logsum = row_max + jnp.log(jnp.sum(jnp.exp(scores - row_max), axis=-1, keepdims=True))
    weights = jnp.exp(scores - logsum).astype(jnp.bfloat16)
    mixed = product("hqk,khd->qhd", weights, split_heads(value)).astype(jnp.bfloat16)
    return (mixed.reshape(query.shape[0], -1), logsum)


def attend_back(query, key_rows, value, heads_out, d_heads, logsum, allowed):
    scores = head_scores(query, key_rows, allowed)
    probs = jnp.exp(scores - logsum)
    probs_low = probs.astype(jnp.bfloat16)
    d_split = split_heads(d_heads)
    d_prob = product("qhd,khd->hqk", d_split, split_heads(value))
    delta = jnp.sum(
        d_split.astype(jnp.float32) * split_heads(heads_out).astype(jnp.float32), axis=-1
    )
    d_score = (probs * (d_prob - jnp.transpose(delta)[:, :, None]) * HEAD_DIM ** (-0.5)).astype(
        jnp.bfloat16
    )
    d_query = product("hqk,khd->qhd", d_score, split_heads(key_rows)).astype(jnp.bfloat16)
    d_key = product("hqk,qhd->khd", d_score, split_heads(query)).astype(jnp.bfloat16)
    d_value = product("hqk,qhd->khd", probs_low, d_split).astype(jnp.bfloat16)
    row_count = query.shape[0]
    return (
        d_query.reshape(row_count, -1),
        d_key.reshape(row_count, -1),
        d_value.reshape(row_count, -1),
    )


def body(
    tokens,
    cotangent,
    seq_lens,
    layer_norm_gain,
    layer_norm_bias,
    w_qkv,
    b_qv,
    w_out,
    b_out,
    w_fc1,
    b_fc1,
    w_fc2,
    b_fc2,
):
    qkv_full, out_full, fc1_full, fc2_full = (
        lax.all_gather(w_qkv, "dp", axis=1, tiled=True),
        lax.all_gather(w_out, "dp", axis=0, tiled=True),
        lax.all_gather(w_fc1, "dp", axis=0, tiled=True),
        lax.all_gather(w_fc2, "dp", axis=0, tiled=True),
    )
    allowed, live_rows = seq_masks(seq_lens, tokens.shape[0])
    input_tokens = tokens.astype(jnp.float32)
    first_normalized, first_centered_scaled, first_inverse_deviation = layer_norm_forward(
        input_tokens, layer_norm_gain[0], layer_norm_bias[0]
    )
    low1 = first_normalized.astype(jnp.bfloat16)
    proj = product("td,idc->itc", low1, qkv_full)
    query = (proj[0] + b_qv[0]).astype(jnp.bfloat16)
    key_rows = proj[1].astype(jnp.bfloat16)
    value = (proj[2] + b_qv[1]).astype(jnp.bfloat16)
    heads_out, logsum = attend(query, key_rows, value, allowed)
    attn_part = product("tc,dc->td", heads_out, out_full)
    attn_mix = lax.psum(attn_part, "tensor")
    first_hidden_state = input_tokens + attn_mix + b_out
    second_normalized, second_centered_scaled, second_inverse_deviation = layer_norm_forward(
        first_hidden_state, layer_norm_gain[1], layer_norm_bias[1]
    )
    low2 = second_normalized.astype(jnp.bfloat16)
    pre_act = jnp.dot(low2, fc1_full, preferred_element_type=jnp.float32) + b_fc1
    act, slope = gelu_parts(pre_act)
    act_low = act.astype(jnp.bfloat16)
    mlp_part = product("tf,df->td", act_low, fc2_full)
    mlp_mix = lax.psum(mlp_part.astype(jnp.bfloat16), "tensor").astype(jnp.float32)
    result = first_hidden_state + mlp_mix + b_fc2
    output = jnp.where(live_rows[:, None], result, 0.0).astype(jnp.bfloat16)
    qkv_back, out_back, fc1_back, fc2_back = (qkv_full, out_full, fc1_full, fc2_full)
    grad_y = jnp.where(live_rows[:, None], cotangent, jnp.zeros_like(cotangent))
    flat_output_gradient = grad_y.astype(jnp.float32)
    d_pre = (jnp.dot(grad_y, fc2_back, preferred_element_type=jnp.float32) * slope).astype(
        jnp.bfloat16
    )
    g_fc2 = product("td,tf->df", grad_y, act_low)
    g_bfc2 = jnp.sum(flat_output_gradient, axis=0)
    g_fc1 = product("td,tf->df", low2, d_pre)
    g_bfc1 = jnp.sum(d_pre.astype(jnp.float32), axis=0)
    d_norm2_part = product("tf,df->td", d_pre, fc1_back)
    second_norm_delta = lax.psum(d_norm2_part.astype(jnp.bfloat16), "tensor").astype(jnp.float32)
    second_gain_gradient = jnp.sum(second_norm_delta * second_centered_scaled, axis=0)
    g_shift2 = jnp.sum(second_norm_delta, axis=0)
    hidden_first_gradient = flat_output_gradient + layer_norm_backward(
        second_norm_delta, layer_norm_gain[1], second_centered_scaled, second_inverse_deviation
    )
    grad_low = hidden_first_gradient.astype(jnp.bfloat16)
    g_out = product("td,tc->dc", grad_low, heads_out)
    g_bout = jnp.sum(hidden_first_gradient, axis=0)
    d_heads = jnp.dot(grad_low, out_back, preferred_element_type=jnp.float32).astype(jnp.bfloat16)
    d_query, d_key, d_value = attend_back(
        query, key_rows, value, heads_out, d_heads, logsum, allowed
    )
    stacked = jnp.stack([d_query, d_key, d_value])
    g_qkv = product("td,itc->idc", low1, stacked)
    g_bqv = jnp.stack(
        [jnp.sum(d_query.astype(jnp.float32), axis=0), jnp.sum(d_value.astype(jnp.float32), axis=0)]
    )
    d_norm1_part = product("itc,idc->td", stacked, qkv_back)
    first_norm_delta = lax.psum(d_norm1_part.astype(jnp.bfloat16), "tensor").astype(jnp.float32)
    first_gain_gradient = jnp.sum(first_norm_delta * first_centered_scaled, axis=0)
    g_shift1 = jnp.sum(first_norm_delta, axis=0)
    input_gradient = hidden_first_gradient + layer_norm_backward(
        first_norm_delta, layer_norm_gain[0], first_centered_scaled, first_inverse_deviation
    )
    shard_qkv, shard_out, shard_fc1, shard_fc2 = (
        lax.psum_scatter(g_qkv, "dp", scatter_dimension=1, tiled=True),
        lax.psum_scatter(g_out, "dp", scatter_dimension=0, tiled=True),
        lax.psum_scatter(g_fc1, "dp", scatter_dimension=0, tiled=True),
        lax.psum_scatter(g_fc2, "dp", scatter_dimension=0, tiled=True),
    )
    gain_sum, shift_sum, bqv_sum, bout_sum, bfc1_sum, bfc2_sum = lax.psum(
        (
            jnp.stack([first_gain_gradient, second_gain_gradient]),
            jnp.stack([g_shift1, g_shift2]),
            g_bqv,
            g_bout,
            g_bfc1,
            g_bfc2,
        ),
        "dp",
    )
    return (
        output,
        input_gradient,
        gain_sum,
        shift_sum,
        shard_qkv,
        bqv_sum,
        shard_out,
        bout_sum,
        shard_fc1,
        bfc1_sum,
        shard_fc2,
        bfc2_sum,
    )


def solution(mesh):
    in_specs = (
        P("dp", None),
        P("dp", None),
        P("dp"),
        P(),
        P(),
        P(None, "dp", "tensor"),
        P(None, "tensor"),
        P("dp", "tensor"),
        P(),
        P("dp", "tensor"),
        P("tensor"),
        P("dp", "tensor"),
        P(),
    )
    out_specs = (
        P("dp", None),
        P("dp", None),
        P(),
        P(),
        P(None, "dp", "tensor"),
        P(None, "tensor"),
        P("dp", "tensor"),
        P(),
        P("dp", "tensor"),
        P("tensor"),
        P("dp", "tensor"),
        P(),
    )
    return jax.shard_map(body, mesh=mesh, in_specs=in_specs, out_specs=out_specs, check_vma=False)
```

profile of v0, /device:TPU:0, one launch (start us, length us, event | category | flops | bytes accessed | tf_op | source)
XLA Modules:
  0.0 795.1 jit_solution(8327538366371572489)
XLA Ops:
  7.2 0.7 all-gather.5.cloned.1.call-update
  8.0 0.7 all-gather.7.cloned.1.call-update
  8.7 1.2 convert_reduce_fusion.3
  9.9 1.3 fusion.23
  11.2 0.8 slice_reduce_fusion.1
  12.2 0.8 fusion.48
  13.0 0.8 fusion.49
  13.8 0.8 reduce-window.4
  14.8 43.7 %all-gather.5.cloned.1.call-done = bf16[3,1024,512]{2,1,0:T(8,128)(2,1)} async-done(((bf16[3,64,512]{2,1,0:T(8,128)(2,1)}), bf16[3,1024,512]{2,1,0:T(8,128)(2,1)}) %all-gather.5.cloned.1.call-update) | async-done | bytes 3145744 | tf_op jit(solution)/shard_map/all_gather | solution.py:109
  58.4 3.1 convolution_bitcast_fusion.1
  61.7 0.2 copy.69
  62.3 0.6 fusion.50
  62.9 0.3 exponential_reduce_fusion
  63.2 0.5 convolution_convert_fusion.6
  63.7 33.1 %all-gather.7.cloned.1.call-done = bf16[1024,512]{1,0:T(8,128)(2,1)} async-done(((bf16[64,512]{1,0:T(8,128)(2,1)}), bf16[1024,512]{1,0:T(8,128)(2,1)}) %all-gather.7.cloned.1.call-update) | async-done | bytes 1048592 | tf_op jit(solution)/shard_map/all_gather | solution.py:110
  96.8 2.7 fusion.51
  99.6 0.5 all-gather.9.cloned.1.call-update
  100.2 0.5 all-gather.11.cloned.1.call-update
  100.8 0.6 slice.34
  101.3 0.6 iota_compare_fusion.2
  102.0 36.8 %all-reduce.8.cloned.1.call-done = f32[256,1024]{1,0:T(8,128)} async-done(((f32[256,1024]{1,0:T(8,128)}), f32[256,1024]{1,0:T(8,128)}) %all-reduce.8.cloned.1.call-update) | async-done | bytes 1048592 | tf_op jit(solution)/shard_map/psum | solution.py:126
  138.8 1.6 fusion.45
  140.4 0.2 multiply_reduce_fusion
  140.7 50.6 %all-gather.9.cloned.1.call-done = bf16[1024,2048]{1,0:T(8,128)(2,1)} async-done(((bf16[64,2048]{1,0:T(8,128)(2,1)}), bf16[1024,2048]{1,0:T(8,128)(2,1)}) %all-gather.9.cloned.1.call-update) | async-done | bytes 4194320 | tf_op jit(solution)/shard_map/all_gather | solution.py:111
  191.2 4.9 convolution_add_fusion
  196.1 46.1 %all-gather.11.cloned.1.call-done = bf16[1024,2048]{1,0:T(8,128)(2,1)} async-done(((bf16[64,2048]{1,0:T(8,128)(2,1)}), bf16[1024,2048]{1,0:T(8,128)(2,1)}) %all-gather.11.cloned.1.call-update) | async-done | bytes 4194320 | tf_op jit(solution)/shard_map/all_gather | solution.py:112
  242.2 5.4 convert_reduce_fusion
  247.6 1.1 copy-done.14
  248.7 2.1 convolution_convert_fusion
  250.8 0.2 all-reduce.14.cloned.1.call-start
  251.0 5.1 convolution_convert_fusion.1
  256.1 22.0 %all-reduce.10.cloned.1.call-done = bf16[256,1024]{1,0:T(8,128)(2,1)} async-done(((bf16[256,1024]{1,0:T(8,128)(2,1)}), bf16[256,1024]{1,0:T(8,128)(2,1)}) %all-reduce.10.cloned.1.call-update) | async-done | bytes 524304 | tf_op jit(solution)/shard_map/psum | solution.py:150
  278.1 1.7 fusion.29
  279.8 1.7 fusion.44
  281.5 1.0 copy-done.1
  282.5 1.1 convolution_convert_fusion.5
  283.6 1.1 copy.73
  284.7 1.1 multiply_reduce_fusion.1
  285.8 1.2 convert_reduce_fusion.5
  287.0 0.8 multiply_convert_fusion
  287.8 0.2 copy-done.4
  288.0 0.4 convolution_convert_fusion.3
  288.5 0.4 convert_reduce_fusion.6
  289.3 3.8 fusion.13
  293.2 3.9 convolution_bitcast_fusion
  297.1 9.4 %copy.82 = f32[3,1024,512]{2,0,1:T(4,128)} copy(f32[3,1024,512]{1,2,0:T(8,128)} %convolution_bitcast_fusion) | data formatting | bytes 12582912 | tf_op jit(solution)/shard_map/td,itc->idc/transpose | solution.py:14
  306.6 1.1 copy-done.2
  307.7 1.9 fusion.34
  309.7 5.9 fusion.43
  315.6 1.0 copy-done.12
  316.6 6.3 fusion.42
  322.9 0.6 copy-done.20
  323.5 0.6 dynamic-slice
  324.9 8.4 %all-reduce.14.cloned.1.call-done = (bf16[256,1024]{1,0:T(8,128)(2,1)}, bf16[256,1024]{1,0:T(8,128)(2,1)}) async-done(((bf16[256,1024]{1,0:T(8,128)(2,1)}, bf16[256,1024]{1,0:T(8,128)(2,1)}), (bf16[256,1024]{1,0:T(8,128)(2,1)}, bf16[256,1024]{1,0:T(8,128)(2,1)})) %all-reduce.14.cloned.1.call-update) | async-done | bytes 1048592 | tf_op jit(solution)/shard_map/psum | solution.py:136
  333.4 1.7 fusion.30
  335.1 64.7 %all-reduce.1 = (f32[2,1024]{1,0:T(2,128)}, f32[2,1024]{1,0:T(2,128)}, f32[2,512]{1,0:T(2,128)}, f32[1024]{0:T(1024)}, f32[2048]{0:T(1024)}, /*index=5*/f32[1024]{0:T(1024)}) all-reduce(f32[2,1024]{1,0:T(2,128)S(1)} %pad_maximum_fusion.3, f32[2,1024]{1,0:T(2,128)S(1)} %pad_maximum_fusion.4, ...), channel_id=1, replica_groups=mesh['dp'=16,'tensor'=2] {'dp'}, use_global_device_ids=true, to_apply=%region_19.20 | all-reduce | flops 9216 | bytes 73728 | tf_op jit(solution)/shard_map/psum | solution.py:181
  399.8 2.0 select_convert_fusion
  401.8 1.4 fusion.22
  403.2 104.7 %all-reduce.12.cloned.1.call-done = f32[3,1024,512]{2,0,1:T(4,128)} async-done(((f32[3,1024,512]{2,0,1:T(4,128)}), f32[3,1024,512]{2,0,1:T(4,128)}) %all-reduce.12.cloned.1.call-update) | async-done | bytes 6291472
  507.8 1.1 constant_dynamic-slice_fusion
  509.0 0.9 copy.83
  509.8 64.0 %reduce-scatter.4.cloned.1.call-done = f32[64,512]{1,0:T(8,128)} async-done(((f32[1024,512]{1,0:T(8,128)}), f32[64,512]{1,0:T(8,128)}) %reduce-scatter.4.cloned.1.call-update) | async-done | bytes 131088 | tf_op jit(solution)/shard_map/reduce_scatter | solution.py:177
  573.8 106.9 %reduce-scatter.6.cloned.1.call-done = f32[64,2048]{1,0:T(8,128)} async-done(((f32[1024,2048]{1,0:T(8,128)}), f32[64,2048]{1,0:T(8,128)}) %reduce-scatter.6.cloned.1.call-update) | async-done | bytes 524304 | tf_op jit(solution)/shard_map/reduce_scatter | solution.py:178
  680.8 107.8 %reduce-scatter.8.cloned.1.call-done = f32[64,2048]{1,0:T(8,128)} async-done(((f32[1024,2048]{1,0:T(8,128)}), f32[64,2048]{1,0:T(8,128)}) %reduce-scatter.8.cloned.1.call-update) | async-done | bytes 524304 | tf_op jit(solution)/shard_map/reduce_scatter | solution.py:179
  (77 shorter events, 2.1 us)
Async XLA Ops:
  7.2 51.3 %all-gather.5.cloned.1.call-start = ((), (), s32[]{:S(2)}) async-start(), calls=%async_computation.3 | async-start | bytes 3342336 | tf_op jit(solution)/shard_map/all_gather | solution.py:109
  7.9 88.9 %all-gather.7.cloned.1.call-start = ((), (), s32[]{:S(2)}) async-start(), calls=%async_computation.4 | async-start | bytes 1114112 | tf_op jit(solution)/shard_map/all_gather | solution.py:110
  8.7 130.1 %all-reduce.8.cloned.1.call-start = ((), (), s32[]{:S(2)}) async-start(), calls=%async_computation.5 | async-start | bytes 2097152 | tf_op jit(solution)/shard_map/psum | solution.py:126
  61.9 1.3 copy-start.5
  62.1 1.1 copy-start.10
  62.3 0.9 copy-start.3
  63.7 38.3 %copy-start.8 = (bf16[8,64,256]{2,1,0:T(8,128)(2,1)}, bf16[8,64,256]{2,1,0:T(8,128)(2,1)S(1)}, u32[]{:S(2)}) copy-start(bf16[8,64,256]{2,1,0:T(8,128)(2,1)S(1)} %convolution_convert_fusion.6) | copy-start | bytes 786436
  63.7 75.1 %copy-start.16 = (f32[1024]{0:T(1024)S(1)}, f32[1024]{0:T(1024)}, u32[]{:S(2)}) copy-start(f32[1024]{0:T(1024)} %param.21) | copy-start | bytes 12292
  99.5 91.7 %copy-start.19 = (f32[2048]{0:T(1024)S(1)}, f32[2048]{0:T(1024)}, u32[]{:S(2)}) copy-start(f32[2048]{0:T(1024)} %param.23) | copy-start | bytes 24580
  99.5 91.7 %all-gather.9.cloned.1.call-start = ((), (), s32[]{:S(2)}) async-start(), calls=%async_computation.6 | async-start | bytes 4456448 | tf_op jit(solution)/shard_map/all_gather | solution.py:111
  100.1 142.1 %all-gather.11.cloned.1.call-start = ((), (), s32[]{:S(2)}) async-start(), calls=%async_computation.7 | async-start | bytes 4456448 | tf_op jit(solution)/shard_map/all_gather | solution.py:112
  100.7 177.4 %all-reduce.10.cloned.1.call-start = ((), (), s32[]{:S(2)}) async-start(), calls=%async_computation.8 | async-start | bytes 1048576 | tf_op jit(solution)/shard_map/psum | solution.py:150
  242.2 6.5 copy-start.18
  247.6 1.1 copy-start.14
  250.8 82.6 %all-reduce.14.cloned.1.call-start = ((), (), s32[]{:S(2)}) async-start(), calls=%async_computation.13 | async-start | bytes 2097152 | tf_op jit(solution)/shard_map/psum | solution.py:136
  278.1 4.4 copy-start.7
  281.5 1.0 copy-start.1
  284.7 2.3 copy-start.6
  287.0 1.0 copy-start.4
  287.0 1.5 copy-start.11
  288.0 1.1 copy-start.15
  289.3 3.9 copy-start
  293.1 214.7 %all-reduce.12.cloned.1.call-start = ((), (), s32[]{:S(2)}) async-start(), calls=%async_computation.12 | async-start | bytes 16777216
  306.5 1.2 copy-start.2
  306.5 1.3 copy-start.9
  306.5 267.3 %reduce-scatter.4.cloned.1.call-start = ((), (), s32[]{:S(2)}) async-start(), calls=%async_computation.9 | async-start | bytes 2228224 | tf_op jit(solution)/shard_map/reduce_scatter | solution.py:177
  309.6 371.1 %reduce-scatter.6.cloned.1.call-start = ((), (), s32[]{:S(2)}) async-start(), calls=%async_computation.10 | async-start | bytes 8912896 | tf_op jit(solution)/shard_map/reduce_scatter | solution.py:178
  315.5 1.0 copy-start.12
  315.6 473.0 %reduce-scatter.8.cloned.1.call-start = ((), (), s32[]{:S(2)}) async-start(), calls=%async_computation.11 | async-start | bytes 8912896 | tf_op jit(solution)/shard_map/reduce_scatter | solution.py:179
  322.9 0.7 copy-start.20
  322.9 76.9 %copy-start.17 = (f32[1024]{0:T(1024)S(1)}, f32[1024]{0:T(1024)}, u32[]{:S(2)}) copy-start(f32[1024]{0:T(1024)} %param.25) | copy-start | bytes 12292
  333.4 68.4 %copy-start.13 = (bf16[256,1024]{1,0:T(8,128)(2,1)S(1)}, bf16[256,1024]{1,0:T(8,128)(2,1)}, u32[]{:S(2)}) copy-start(bf16[256,1024]{1,0:T(8,128)(2,1)} %get-tuple-element.77) | copy-start | bytes 1572868
Sparse Core Ops, SparseCore 0:
  10.2 48.2 all-gather.4
  60.6 36.1 all-gather.6
  99.7 39.0 all-reduce.7
  140.8 50.3 all-gather.8
  193.2 48.8 all-gather.10
  250.9 27.1 all-reduce.9
  293.2 40.0 all-reduce.13
  337.1 170.6 all-reduce.11
  512.1 61.6 reduce-scatter.3
  578.3 102.3 reduce-scatter.5
  685.4 103.0 reduce-scatter.7
where the time goes:
time: 796 us; the launch traced here: 795 us
  waiting for transfers between devices  627 us (79%)
  blocking collectives  64.7 us (8%)
  matrix products  49.9 us (6%)
  local copies, waits for them, and re-layouts  22.4 us (3%)
  other arithmetic  15.9 us (2%)
  between operations  14.9 us (2%)
    reduce_scatter x1, waiting for transfers between devices, body(): lax.psum_scatter(g_fc2, 'dp', scatter_dimension=0, tiled=True)  108 us
    unnamed x12, waiting for transfers between devices  107 us
    reduce_scatter x1, waiting for transfers between devices, body(): lax.psum_scatter(g_fc1, 'dp', scatter_dimension=0, tiled=True)  107 us
    psum x1, blocking collectives, body(): lax.psum((jnp.stack([first_gain_gradient, second_gain_gradient]), jnp.sta...  64.7 us
    reduce_scatter x1, waiting for transfers between devices, body(): lax.psum_scatter(g_out, 'dp', scatter_dimension=0, tiled=True)  64 us
    all_gather x1, waiting for transfers between devices, body(): lax.all_gather(w_fc1, 'dp', axis=0, tiled=True)  50.6 us
    all_gather x1, waiting for transfers between devices, body(): lax.all_gather(w_fc2, 'dp', axis=0, tiled=True)  46.1 us
    all_gather x1, waiting for transfers between devices, body(): lax.all_gather(w_qkv, 'dp', axis=1, tiled=True)  43.7 us
  transfers between devices with their start and end apart: 11, of which 11 were waited for; matrix products, arithmetic and copies ran while one was open for 7% of the time, Pallas kernels for 0%

commit v1 on v0

--- a/solution.py
+++ b/solution.py
@@ -88,6 +88,19 @@
         d_key.reshape(row_count, -1),
         d_value.reshape(row_count, -1),
     )
+
+
+def sum_tensor(part):
+    low = lax.optimization_barrier(part.astype(jnp.bfloat16))
+    count = lax.axis_size("tensor")
+    if count != 2:
+        return lax.psum(low, "tensor").astype(jnp.float32)
+    other = lax.ppermute(low, "tensor", [(0, 1), (1, 0)])
+    return low.astype(jnp.float32) + other.astype(jnp.float32)
+
+
+def sum_dp(vectors):
+    return lax.psum(vectors, "dp")
 
 
 def body(
@@ -105,25 +118,26 @@
     w_fc2,
     b_fc2,
 ):
-    qkv_full, out_full, fc1_full, fc2_full = (
-        lax.all_gather(w_qkv, "dp", axis=1, tiled=True),
-        lax.all_gather(w_out, "dp", axis=0, tiled=True),
-        lax.all_gather(w_fc1, "dp", axis=0, tiled=True),
-        lax.all_gather(w_fc2, "dp", axis=0, tiled=True),
-    )
+    heads_width, hidden_width = w_out.shape[1], w_fc1.shape[1]
+    attn_shards = jnp.concatenate([w_qkv[0], w_qkv[1], w_qkv[2], w_out], axis=1)
+    mlp_shards = jnp.concatenate([w_fc1, w_fc2], axis=1)
+    attn_full = lax.all_gather(attn_shards, "dp", axis=0, tiled=True)
+    mlp_full = lax.all_gather(mlp_shards, "dp", axis=0, tiled=True)
+    qkv_full, out_full = attn_full[:, : 3 * heads_width], attn_full[:, 3 * heads_width :]
+    fc1_full, fc2_full = mlp_full[:, :hidden_width], mlp_full[:, hidden_width:]
     allowed, live_rows = seq_masks(seq_lens, tokens.shape[0])
     input_tokens = tokens.astype(jnp.float32)
     first_normalized, first_centered_scaled, first_inverse_deviation = layer_norm_forward(
         input_tokens, layer_norm_gain[0], layer_norm_bias[0]
     )
     low1 = first_normalized.astype(jnp.bfloat16)
-    proj = product("td,idc->itc", low1, qkv_full)
-    query = (proj[0] + b_qv[0]).astype(jnp.bfloat16)
-    key_rows = proj[1].astype(jnp.bfloat16)
-    value = (proj[2] + b_qv[1]).astype(jnp.bfloat16)
+    proj = product("td,dc->tc", low1, qkv_full)
+    query = (proj[:, :heads_width] + b_qv[0]).astype(jnp.bfloat16)
+    key_rows = proj[:, heads_width : 2 * heads_width].astype(jnp.bfloat16)
+    value = (proj[:, 2 * heads_width :] + b_qv[1]).astype(jnp.bfloat16)
     heads_out, logsum = attend(query, key_rows, value, allowed)
     attn_part = product("tc,dc->td", heads_out, out_full)
-    attn_mix = lax.psum(attn_part, "tensor")
+    attn_mix = sum_tensor(attn_part)
     first_hidden_state = input_tokens + attn_mix + b_out
     second_normalized, second_centered_scaled, second_inverse_deviation = layer_norm_forward(
         first_hidden_state, layer_norm_gain[1], layer_norm_bias[1]
@@ -133,7 +147,7 @@
     act, slope = gelu_parts(pre_act)
     act_low = act.astype(jnp.bfloat16)
     mlp_part = product("tf,df->td", act_low, fc2_full)
-    mlp_mix = lax.psum(mlp_part.astype(jnp.bfloat16), "tensor").astype(jnp.float32)
+    mlp_mix = sum_tensor(mlp_part)
     result = first_hidden_state + mlp_mix + b_fc2
     output = jnp.where(live_rows[:, None], result, 0.0).astype(jnp.bfloat16)
     qkv_back, out_back, fc1_back, fc2_back = (qkv_full, out_full, fc1_full, fc2_full)
@@ -145,9 +159,11 @@
     g_fc2 = product("td,tf->df", grad_y, act_low)
     g_bfc2 = jnp.sum(flat_output_gradient, axis=0)
     g_fc1 = product("td,tf->df", low2, d_pre)
+    g_mlp = jnp.concatenate([g_fc1.astype(jnp.bfloat16), g_fc2.astype(jnp.bfloat16)], axis=1)
+    shard_mlp = lax.psum_scatter(g_mlp, "dp", scatter_dimension=0, tiled=True)
     g_bfc1 = jnp.sum(d_pre.astype(jnp.float32), axis=0)
     d_norm2_part = product("tf,df->td", d_pre, fc1_back)
-    second_norm_delta = lax.psum(d_norm2_part.astype(jnp.bfloat16), "tensor").astype(jnp.float32)
+    second_norm_delta = sum_tensor(d_norm2_part)
     second_gain_gradient = jnp.sum(second_norm_delta * second_centered_scaled, axis=0)
     g_shift2 = jnp.sum(second_norm_delta, axis=0)
     hidden_first_gradient = flat_output_gradient + layer_norm_backward(
@@ -160,35 +176,43 @@
     d_query, d_key, d_value = attend_back(
         query, key_rows, value, heads_out, d_heads, logsum, allowed
     )
-    stacked = jnp.stack([d_query, d_key, d_value])
-    g_qkv = product("td,itc->idc", low1, stacked)
+    stacked = jnp.concatenate([d_query, d_key, d_value], axis=1)
+    g_qkv = product("td,tc->dc", low1, stacked)
+    g_attn = jnp.concatenate([g_qkv.astype(jnp.bfloat16), g_out.astype(jnp.bfloat16)], axis=1)
+    shard_attn = lax.psum_scatter(g_attn, "dp", scatter_dimension=0, tiled=True)
     g_bqv = jnp.stack(
         [jnp.sum(d_query.astype(jnp.float32), axis=0), jnp.sum(d_value.astype(jnp.float32), axis=0)]
     )
-    d_norm1_part = product("itc,idc->td", stacked, qkv_back)
-    first_norm_delta = lax.psum(d_norm1_part.astype(jnp.bfloat16), "tensor").astype(jnp.float32)
+    d_norm1_part = product("tc,dc->td", stacked, qkv_back)
+    first_norm_delta = sum_tensor(d_norm1_part)
     first_gain_gradient = jnp.sum(first_norm_delta * first_centered_scaled, axis=0)
     g_shift1 = jnp.sum(first_norm_delta, axis=0)
     input_gradient = hidden_first_gradient + layer_norm_backward(
         first_norm_delta, layer_norm_gain[0], first_centered_scaled, first_inverse_deviation
     )
-    shard_qkv, shard_out, shard_fc1, shard_fc2 = (
-        lax.psum_scatter(g_qkv, "dp", scatter_dimension=1, tiled=True),
-        lax.psum_scatter(g_out, "dp", scatter_dimension=0, tiled=True),
-        lax.psum_scatter(g_fc1, "dp", scatter_dimension=0, tiled=True),
-        lax.psum_scatter(g_fc2, "dp", scatter_dimension=0, tiled=True),
-    )
-    gain_sum, shift_sum, bqv_sum, bout_sum, bfc1_sum, bfc2_sum = lax.psum(
-        (
-            jnp.stack([first_gain_gradient, second_gain_gradient]),
-            jnp.stack([g_shift1, g_shift2]),
-            g_bqv,
+    shard_attn, shard_mlp = shard_attn.astype(jnp.float32), shard_mlp.astype(jnp.float32)
+    shard_qkv = jnp.stack([shard_attn[:, i * heads_width : (i + 1) * heads_width] for i in range(3)])
+    shard_out = shard_attn[:, 3 * heads_width :]
+    shard_fc1, shard_fc2 = shard_mlp[:, :hidden_width], shard_mlp[:, hidden_width:]
+    vectors = jnp.concatenate(
+        [
+            first_gain_gradient,
+            second_gain_gradient,
+            g_shift1,
+            g_shift2,
+            g_bqv.reshape(-1),
             g_bout,
             g_bfc1,
             g_bfc2,
-        ),
-        "dp",
-    )
+        ]
+    )
+    vectors = sum_dp(vectors)
+    width = tokens.shape[1]
+    cuts = [2 * width, 4 * width, 4 * width + 2 * heads_width]
+    cuts += [cuts[-1] + width, cuts[-1] + width + hidden_width]
+    gain_sum, shift_sum, bqv_sum, bout_sum, bfc1_sum, bfc2_sum = jnp.split(vectors, cuts)
+    gain_sum, shift_sum = gain_sum.reshape(2, width), shift_sum.reshape(2, width)
+    bqv_sum = bqv_sum.reshape(2, heads_width)
     return (
         output,
         input_gradient,

time: 796 us -> 375 us (0.47)
  waiting for transfers between devices: 627 us -> 227 us
  matrix products: 49.9 us -> 31.9 us
  local copies, waits for them, and re-layouts: 22.4 us -> 13.9 us
    reduce_scatter x3 -> x2, waiting for transfers between devices: 279 us -> 77.4 us  [the longest x1 77.4 us: body(): shard_mlp = lax.psum_scatter(g_mlp, 'dp', scatter_dimension=0, tiled=True)]
    unnamed x12 -> x4, waiting for transfers between devices: 107 us -> 0.07 us
    all_gather x4 -> x2, waiting for transfers between devices: 173 us -> 105 us  [the longest x1 54.1 us: body(): mlp_full = lax.all_gather(mlp_shards, 'dp', axis=0, tiled=True)]
    psum x3 -> x0, waiting for transfers between devices: 67.2 us -> none  [the longest x1 36.8 us: body(): attn_mix = lax.psum(attn_part, 'tensor')]
    ppermute x0 -> x4, waiting for transfers between devices: none -> 44.1 us  [sum_tensor(): other = lax.ppermute(low, 'tensor', [(0, 1), (1, 0)])]
    dot_general x15, matrix products: 38.5 us -> 23.6 us  [product(): return jnp.einsum(spec, left, right, preferred_element_type=jnp.float32)]
    concatenate x0 -> x4, other arithmetic: none -> 14.3 us  [the longest x1 8.25 us: body(): jnp.concatenate([g_fc1.astype(jnp.bfloat16), g_fc2.astype(jnp.bfloat16)],...]
    transpose x1 -> x0, local copies, waits for them, and re-layouts: 9.37 us -> none  [product(): return jnp.einsum(spec, left, right, preferred_element_type=jnp.float32)]
  transfers between devices with their start and end apart: 11 -> 8, of which waited for: 11 -> 7; matrix products, arithmetic and copies ran while one was open for 7% -> 11% of each run, Pallas kernels for 0% -> 0%
where the time goes in v1:
time: 375 us
  waiting for transfers between devices  227 us (61%)
  blocking collectives  58.6 us (16%)
  matrix products  31.9 us (9%)
  other arithmetic  23.8 us (6%)
  between operations  14.4 us (4%)
  local copies, waits for them, and re-layouts  13.9 us (4%)
  starting transfers between devices  5.41 us (1%)
    reduce_scatter x1, waiting for transfers between devices, body(): shard_mlp = lax.psum_scatter(g_mlp, 'dp', scatter_dimension=0, tiled=True)  77.4 us
    psum x1, blocking collectives, sum_dp(): return lax.psum(vectors, 'dp')  58.6 us
    all_gather x1, waiting for transfers between devices, body(): mlp_full = lax.all_gather(mlp_shards, 'dp', axis=0, tiled=True)  54.1 us
    all_gather x1, waiting for transfers between devices, body(): attn_full = lax.all_gather(attn_shards, 'dp', axis=0, tiled=True)  51.2 us
    ppermute x4, waiting for transfers between devices, sum_tensor(): other = lax.ppermute(low, 'tensor', [(0, 1), (1, 0)])  44.1 us
    dot_general x15, matrix products, product(): return jnp.einsum(spec, left, right, preferred_element_type=jnp.float32)  23.6 us
    concatenate x1, other arithmetic, body(): jnp.concatenate([g_fc1.astype(jnp.bfloat16), g_fc2.astype(jnp.bfloat16)],...  8.25 us
  transfers between devices with their start and end apart: 8, of which 7 were waited for; matrix products, arithmetic and copies ran while one was open for 11% of the time, Pallas kernels for 0%

profile of v1, /device:TPU:0, one launch (start us, length us, event | category | flops | bytes accessed | tf_op | source)
XLA Modules:
  0.0 374.8 jit_solution(1021533827294372795)
XLA Ops:
  7.3 1.0 slice_bitcast_fusion.5
  8.2 1.6 pad_maximum_fusion.7
  9.9 1.9 pad_maximum_fusion.3
  11.8 0.2 reduce-window.4
  12.1 0.1 convert_reduce_fusion.1
  12.2 0.3 fusion.49
  12.7 51.2 %all-gather.3.cloned.1.call-done = bf16[1024,2048]{1,0:T(8,128)(2,1)} async-done(((bf16[64,2048]{1,0:T(8,128)(2,1)}), bf16[1024,2048]{1,0:T(8,128)(2,1)}) %all-gather.3.cloned.1.call-update) | async-done | bytes 4194320 | tf_op jit(solution)/shard_map/all_gather | solution.py:124
  63.9 3.0 fusion.10
  67.0 0.1 copy.49
  67.5 0.5 fusion.79
  68.0 0.3 exponential_reduce_fusion
  68.4 0.5 convolution_convert_fusion.9
  68.8 1.8 convolution_convert_fusion.4
  70.7 1.5 collective-permute-start
  72.2 0.6 slice.97
  72.8 0.7 iota_compare_fusion.2
  73.5 11.3 %collective-permute-done = bf16[256,1024]{1,0:T(8,128)(2,1)S(1)} collective-permute-done((bf16[256,1024]{1,0:T(8,128)(2,1)S(1)}, bf16[256,1024]{1,0:T(8,128)(2,1)S(1)}, u32[]{:S(2)}, u32[]{:S(2)}) %collective-permute-start) | collective-permute-done | bytes 524320 | tf_op jit(solution)/shard_map/ppermute | solution.py:98
  84.8 0.3 fusion.71
  85.1 0.3 multiply_reduce_fusion.2
  85.4 54.1 %all-gather.5.cloned.1.call-done = bf16[1024,4096]{1,0:T(8,128)(2,1)} async-done(((bf16[64,4096]{1,0:T(8,128)(2,1)}), bf16[1024,4096]{1,0:T(8,128)(2,1)}) %all-gather.5.cloned.1.call-update) | async-done | bytes 8388624 | tf_op jit(solution)/shard_map/all_gather | solution.py:125
  139.5 3.7 fusion.12
  143.2 1.1 copy-done.25
  144.3 2.3 convert_reduce_fusion
  146.6 1.4 fusion.30
  148.0 1.5 collective-permute-start.2
  149.6 1.5 fusion.33
  151.1 0.6 collective-permute-start.1
  151.7 11.2 %collective-permute-done.2 = bf16[256,1024]{1,0:T(8,128)(2,1)S(1)} collective-permute-done((bf16[256,1024]{1,0:T(8,128)(2,1)S(1)}, bf16[256,1024]{1,0:T(8,128)(2,1)S(1)}, u32[]{:S(2)}, u32[]{:S(2)}) %collective-permute-start.2) | collective-permute-done | bytes 524320 | tf_op jit(solution)/shard_map/ppermute | solution.py:98
  162.9 0.6 multiply_reduce_fusion
  163.5 9.9 %collective-permute-done.1 = bf16[256,1024]{1,0:T(8,128)(2,1)S(1)} collective-permute-done((bf16[256,1024]{1,0:T(8,128)(2,1)S(1)}, bf16[256,1024]{1,0:T(8,128)(2,1)S(1)}, u32[]{:S(2)}, u32[]{:S(2)}) %collective-permute-start.1) | collective-permute-done | bytes 524320 | tf_op jit(solution)/shard_map/ppermute | solution.py:98
  173.4 1.6 fusion.70
  175.0 1.0 copy-done
  176.0 2.4 convolution_convert_fusion.8
  178.3 1.1 copy.52
  179.4 1.1 multiply_reduce_fusion.3
  180.5 0.7 convert_reduce_fusion.3
  181.2 0.7 multiply_convert_fusion
  181.9 0.3 copy-done.12
  182.2 0.4 convolution_convert_fusion.6
  182.7 0.4 convert_reduce_fusion.4
  183.1 0.4 copy-done.1
  183.5 0.5 convolution_convert_fusion.3
  184.0 1.2 convolution_convert_fusion
  185.2 2.6 pad_maximum_fusion.1
  187.9 4.7 %convolution_convert_fusion.2 = bf16[1024,2048]{1,0:T(8,128)(2,1)} fusion(bf16[256,2048]{1,0:T(8,128)(2,1)} %copy-done.13, f32[256,1024]{1,0:T(8,128)S(1)} %get-tuple-element.23, f32[1024]{0:T(1024)S(1)} %bitcast.80, f32[1024]{0:T(1024)S(1)} %bitcast.78, f32[256]{0:T(256)S(1)} %add_rsqrt_fusion, f32[256]{0:T(256)S(1)} %broadcast_multiply_fusion.4), kind=kOutput, calls=%fused_computation.4 | convolution fusion | flops 1077149696 | bytes 6301696 | tf_op jit(solution)/shard_map/td,tf->df/dot_general | solution.py:14
  192.7 3.4 convolution_convert_fusion.1
  196.1 8.3 %pad_maximum_fusion = bf16[1024,4096]{1,0:T(8,128)(2,1)} fusion(bf16[1024,2048]{1,0:T(8,128)(2,1)} %convolution_convert_fusion.1, bf16[1024,2048]{1,0:T(8,128)(2,1)} %convolution_convert_fusion.2), kind=kLoop, calls=%fused_computation | loop fusion | flops 16777216 | bytes 16777216 | tf_op jit(solution)/shard_map/concatenate | solution.py:162
  204.4 0.9 copy-done.17
  205.4 3.0 fusion.27
  208.4 1.5 collective-permute-start.3
  210.2 11.6 %collective-permute-done.3 = bf16[256,1024]{1,0:T(8,128)(2,1)S(1)} collective-permute-done((bf16[256,1024]{1,0:T(8,128)(2,1)S(1)}, bf16[256,1024]{1,0:T(8,128)(2,1)S(1)}, u32[]{:S(2)}, u32[]{:S(2)}) %collective-permute-start.3) | collective-permute-done | bytes 524320 | tf_op jit(solution)/shard_map/ppermute | solution.py:98
  221.8 0.6 fusion.48
  222.5 58.6 %psum.7 = f32[9216]{0:T(1024)S(1)} all-reduce(f32[9216]{0:T(1024)S(1)} %constant_dynamic-update-slice_fusion), channel_id=1, replica_groups=mesh['dp'=16,'tensor'=2] {'dp'}, use_global_device_ids=true, to_apply=%region_22.23 | all-reduce | flops 9216 | bytes 73728 | tf_op jit(solution)/shard_map/psum | solution.py:103
  281.0 0.6 fusion.74
  281.6 0.6 split.29
  282.2 0.6 fusion.75
  282.8 0.6 split.27
  283.4 0.6 split.25
  284.1 1.4 fusion.47
  285.5 1.5 slice.130
  287.0 1.0 convert_element_type.180
  288.0 0.8 pad_maximum_fusion.4
  288.8 77.4 %reduce-scatter.5.cloned.1.call-done = bf16[64,4096]{1,0:T(8,128)(2,1)} async-done(((bf16[1024,4096]{1,0:T(8,128)(2,1)}), bf16[64,4096]{1,0:T(8,128)(2,1)}) %reduce-scatter.5.cloned.1.call-update) | async-done | bytes 524304 | tf_op jit(solution)/shard_map/reduce_scatter | solution.py:163
  366.1 2.1 fusion.73
  (94 shorter events, 1.4 us)
Async XLA Ops:
  7.2 4.6 %copy-start.27 = (s32[4]{0:T(128)S(1)}, s32[4]{0:T(128)}, u32[]{:S(2)}) copy-start(s32[4]{0:T(128)} %param.15) | copy-start | bytes 52
  7.2 4.9 %copy-start.2 = (bf16[256,1024]{1,0:T(8,128)(2,1)S(1)}, bf16[256,1024]{1,0:T(8,128)(2,1)}, u32[]{:S(2)}) copy-start(bf16[256,1024]{1,0:T(8,128)(2,1)} %param.13) | copy-start | bytes 1572868
  7.2 5.3 %copy-start.24 = (f32[2,512]{1,0:T(2,128)S(1)}, f32[2,512]{1,0:T(2,128)}, u32[]{:S(2)}) copy-start(f32[2,512]{1,0:T(2,128)} %param.19) | copy-start | bytes 12292
  7.2 5.4 %copy-start.20 = (f32[2,1024]{1,0:T(2,128)S(1)}, f32[2,1024]{1,0:T(2,128)}, u32[]{:S(2)}) copy-start(f32[2,1024]{1,0:T(2,128)} %param.16) | copy-start | bytes 24580
  7.2 5.4 %copy-start.21 = (f32[2,1024]{1,0:T(2,128)S(1)}, f32[2,1024]{1,0:T(2,128)}, u32[]{:S(2)}) copy-start(f32[2,1024]{1,0:T(2,128)} %param.17) | copy-start | bytes 24580
  7.2 56.7 %all-gather.3.cloned.1.call-start = ((), (), s32[]{:S(2)}) async-start(), calls=%async_computation.2 | async-start | bytes 4456448 | tf_op jit(solution)/shard_map/all_gather | solution.py:124
  9.8 129.7 %all-gather.5.cloned.1.call-start = ((), (), s32[]{:S(2)}) async-start(), calls=%async_computation.3 | async-start | bytes 8912896 | tf_op jit(solution)/shard_map/all_gather | solution.py:125
  11.8 273.7 %reduce-scatter.3.cloned.1.call-start = ((), (), s32[]{:S(2)}) async-start(), calls=%async_computation.4 | async-start | bytes 4456448 | tf_op jit(solution)/shard_map/reduce_scatter | solution.py:182
  67.2 1.1 copy-start.11
  67.3 1.0 copy-start.9
  67.5 0.9 copy-start.5
  68.4 16.5 %copy-start.3 = (bf16[256,1024]{1,0:T(8,128)(2,1)S(1)}, bf16[256,1024]{1,0:T(8,128)(2,1)}, u32[]{:S(2)}) copy-start(bf16[256,1024]{1,0:T(8,128)(2,1)} %param.13) | copy-start | bytes 1572868
  68.4 16.4 %copy-start.22 = (f32[1024]{0:T(1024)S(1)}, f32[1024]{0:T(1024)}, u32[]{:S(2)}) copy-start(f32[1024]{0:T(1024)} %param.21) | copy-start | bytes 12292
  68.8 4.6 %copy-start.7 = (bf16[8,64,256]{2,1,0:T(8,128)(2,1)}, bf16[8,64,256]{2,1,0:T(8,128)(2,1)S(1)}, u32[]{:S(2)}) copy-start(bf16[8,64,256]{2,1,0:T(8,128)(2,1)S(1)} %convolution_convert_fusion.9) | copy-start | bytes 786436
  70.7 68.8 %copy-start.26 = (f32[2048]{0:T(1024)S(1)}, f32[2048]{0:T(1024)}, u32[]{:S(2)}) copy-start(f32[2048]{0:T(1024)} %param.23) | copy-start | bytes 24580
  70.7 14.1 %collective-permute-start = (bf16[256,1024]{1,0:T(8,128)(2,1)S(1)}, bf16[256,1024]{1,0:T(8,128)(2,1)S(1)}, u32[]{:S(2)}, u32[]{:S(2)}) collective-permute-start(bf16[256,1024]{1,0:T(8,128)(2,1)S(1)} %convolution_convert_fusion.4), channel_id=1, source_target_pairs={{0,1},{1,0},{2,3},{3,2},{4,5},{5,4},{6,7},{7,6},{8,9},{9,8},{10,11... | collective-permute-start | bytes 1572872 | tf_op jit(solution)/shard_map/ppermute | solution.py:98
  139.5 3.7 copy-start.14
  139.5 4.8 %copy-start.25 = (bf16[1024,4096]{1,0:T(8,128)(2,1)S(1)}, bf16[1024,4096]{1,0:T(8,128)(2,1)}, u32[]{:S(2)}) copy-start(bf16[1024,4096]{1,0:T(8,128)(2,1)} %all-gather.5.cloned.1.call-done) | copy-start | bytes 25165828
  144.3 5.2 %copy-start.28 = (f32[256,2048]{1,0:T(8,128)}, f32[256,2048]{1,0:T(8,128)S(1)}, u32[]{:S(2)}) copy-start(f32[256,2048]{1,0:T(8,128)S(1)} %fusion.12) | copy-start | bytes 6291460
  146.6 1.4 copy-start.13
  148.0 14.9 %collective-permute-start.2 = (bf16[256,1024]{1,0:T(8,128)(2,1)S(1)}, bf16[256,1024]{1,0:T(8,128)(2,1)S(1)}, u32[]{:S(2)}, u32[]{:S(2)}) collective-permute-start(bf16[256,1024]{1,0:T(8,128)(2,1)S(1)} %fusion.30), channel_id=1, source_target_pairs={{0,1},{1,0},{2,3},{3,2},{4,5},{5,4},{6,7},{7,6},{8,9},{9,8},{10,11... | collective-permute-start | bytes 1572872 | tf_op jit(solution)/shard_map/ppermute | solution.py:98
  151.0 22.4 %copy-start.23 = (f32[1024]{0:T(1024)S(1)}, f32[1024]{0:T(1024)}, u32[]{:S(2)}) copy-start(f32[1024]{0:T(1024)} %param.25) | copy-start | bytes 12292
  151.1 22.4 %collective-permute-start.1 = (bf16[256,1024]{1,0:T(8,128)(2,1)S(1)}, bf16[256,1024]{1,0:T(8,128)(2,1)S(1)}, u32[]{:S(2)}, u32[]{:S(2)}) collective-permute-start(bf16[256,1024]{1,0:T(8,128)(2,1)S(1)} %fusion.33), channel_id=1, source_target_pairs={{0,1},{1,0},{2,3},{3,2},{4,5},{5,4},{6,7},{7,6},{8,9},{9,8},{10,11... | collective-permute-start | bytes 1572872 | tf_op jit(solution)/shard_map/ppermute | solution.py:98
  175.0 1.0 copy-start
  179.4 1.8 copy-start.6
  181.2 2.8 copy-start.16
  181.2 1.0 copy-start.12
  181.2 1.5 copy-start.10
  182.2 1.2 copy-start.1
  182.2 1.3 copy-start.8
  182.7 1.3 copy-start.4
  183.5 1.7 copy-start.18
  187.9 4.8 %copy-start.15 = (bf16[256,1024]{1,0:T(8,128)(2,1)S(1)}, bf16[256,1024]{1,0:T(8,128)(2,1)}, u32[]{:S(2)}) copy-start(bf16[256,1024]{1,0:T(8,128)(2,1)} %param.14) | copy-start | bytes 1572868
  187.9 178.3 %reduce-scatter.5.cloned.1.call-start = ((), (), s32[]{:S(2)}) async-start(), calls=%async_computation.5 | async-start | bytes 8912896 | tf_op jit(solution)/shard_map/reduce_scatter | solution.py:163
  187.9 4.7 %copy-start.29 = (f32[256,2048]{1,0:T(8,128)S(1)}, f32[256,2048]{1,0:T(8,128)}, u32[]{:S(2)}) copy-start(f32[256,2048]{1,0:T(8,128)} %copy-done.28) | copy-start | bytes 6291460
  204.3 1.0 copy-start.17
  204.3 1.0 copy-start.19
  208.4 13.3 %collective-permute-start.3 = (bf16[256,1024]{1,0:T(8,128)(2,1)S(1)}, bf16[256,1024]{1,0:T(8,128)(2,1)S(1)}, u32[]{:S(2)}, u32[]{:S(2)}) collective-permute-start(bf16[256,1024]{1,0:T(8,128)(2,1)S(1)} %fusion.27), channel_id=1, source_target_pairs={{0,1},{1,0},{2,3},{3,2},{4,5},{5,4},{6,7},{7,6},{8,9},{9,8},{10,11... | collective-permute-start | bytes 1572872 | tf_op jit(solution)/shard_map/ppermute | solution.py:98
Sparse Core Ops, SparseCore 0:
  10.8 53.0 all-gather.2
  66.6 72.8 all-gather.4
  188.0 71.6 reduce-scatter.2
  263.6 102.4 reduce-scatter.4

commit v2 on v1

--- a/solution.py
+++ b/solution.py
@@ -1,6 +1,8 @@
 import jax
 import jax.numpy as jnp
 from jax import lax
+from jax.experimental import pallas as pl
+from jax.experimental.pallas import tpu as pltpu
 from jax.sharding import PartitionSpec as P
 
 HEAD_DIM = 64
@@ -99,8 +101,212 @@
     return low.astype(jnp.float32) + other.astype(jnp.float32)
 
 
-def sum_dp(vectors):
-    return lax.psum(vectors, "dp")
+def chip_at(place, chips):
+    place = (place + chips) % chips
+    back = place // (chips // 2)
+    return 2 * (place * (1 - back) + (chips - 1 - place) * back) + back
+
+
+def ring_place(chips):
+    device = lax.axis_index("dp")
+    core, chip = device % 2, device // 2
+    column, row = chip % 2, chip // 2
+    place = row * (1 - column) + (chips - 1 - row) * column
+    return device, chip, core, place
+
+
+def send(source, target, send_sem, recv_sem, device):
+    return pltpu.make_async_remote_copy(
+        src_ref=source,
+        dst_ref=target,
+        send_sem=send_sem,
+        recv_sem=recv_sem,
+        device_id={"dp": device},
+        device_id_type=pl.DeviceIdType.MESH,
+    )
+
+
+def meet(devices):
+    barrier = pltpu.get_barrier_semaphore()
+    for device in devices:
+        pl.semaphore_signal(
+            barrier, inc=1, device_id={"dp": device}, device_id_type=pl.DeviceIdType.MESH
+        )
+    pl.semaphore_wait(barrier, len(devices))
+
+
+def gather_kernel(chips, own, out, rs, rr, ls, lr, ps, pr, own_sem):
+    device, chip, core, place = ring_place(chips)
+    right = 2 * chip_at(place + 1, chips) + core
+    left = 2 * chip_at(place - 1, chips) + core
+    partner = 2 * chip + 1 - core
+    meet((right, left, partner))
+    top, width = chips // 2, own.shape[1]
+    half = width // 2
+
+    def block(step, whose, hop, side):
+        at = out.at[2 * chip_at(place + step, chips) + whose]
+        if hop < top:
+            return at
+        return at.at[:, pl.ds(side * half, half)]
+
+    started = []
+
+    def go(copy):
+        copy.start()
+        started.append(copy)
+
+    go(send(own, out.at[device], rs.at[0], rr.at[0], right))
+    go(send(own, out.at[device], ls.at[0], lr.at[0], left))
+    go(send(own, out.at[device], ps.at[0], pr.at[0], partner))
+    keep = pltpu.make_async_copy(own, out.at[device], own_sem)
+    keep.start()
+    passed = [block(0, 1 - core, 0, 0)]
+    for hop in range(1, top + 1):
+        for side, sign, s_sem, r_sem, onward in ((0, -1, rs, rr, right), (1, 1, ls, lr, left)):
+            here = block(sign * hop, core, hop, side)
+            send(here, here, s_sem.at[hop - 1], r_sem.at[hop - 1], onward).wait_recv()
+            if hop < top:
+                part = block(sign * hop, core, hop + 1, side)
+                go(send(part, part, s_sem.at[hop], r_sem.at[hop], onward))
+            slot = len(passed)
+            go(send(here, here, ps.at[slot], pr.at[slot], partner))
+            passed.append(block(sign * hop, 1 - core, hop, side))
+    for slot, here in enumerate(passed):
+        send(here, here, ps.at[slot], pr.at[slot], partner).wait_recv()
+    for copy in started:
+        copy.wait_send()
+    keep.wait()
+
+
+def gather_rows(shard):
+    count = lax.axis_size("dp")
+    chips = count // 2
+    top = chips // 2
+    dma = pltpu.SemaphoreType.DMA
+    out = pl.pallas_call(
+        lambda *refs: gather_kernel(chips, *refs),
+        out_shape=jax.ShapeDtypeStruct((count, *shard.shape), shard.dtype),
+        in_specs=[pl.BlockSpec(memory_space=pltpu.VMEM)],
+        out_specs=pl.BlockSpec(memory_space=pl.ANY),
+        scratch_shapes=[dma((top,))] * 4 + [dma((chips + 1,))] * 2 + [dma],
+        compiler_params=pltpu.CompilerParams(collective_id=0, has_side_effects=True),
+        name="gather_rows",
+    )(shard)
+    return out.reshape(count * shard.shape[0], shard.shape[1])
+
+
+def scatter_kernel(
+    chips, grads, vec, out, vec_out,
+    pbuf, rbuf, lbuf, rstage, lstage, vpart, vslots,
+    ps, pr, rs, rr, ls, lr, vps, vpr, vrs, vrr, vls, vlr,
+):
+    device, chip, core, place = ring_place(chips)
+    right = 2 * chip_at(place + 1, chips) + core
+    left = 2 * chip_at(place - 1, chips) + core
+    partner = 2 * chip + 1 - core
+    meet((right, left, partner))
+    top, width = chips // 2, out.shape[1]
+    half = width // 2
+    low, high = pl.ds(0, half), pl.ds(half, half)
+    started = []
+
+    def go(copy):
+        copy.start()
+        started.append(copy)
+
+    order = [top]
+    for step in range(1, top):
+        order += [top - step, step - top]
+    order.append(0)
+    go(send(vec, vpart, vps.at[0], vpr.at[0], partner))
+    for slot, step in enumerate(order):
+        mine = grads.at[2 * chip_at(place + step, chips) + 1 - core]
+        go(send(mine, pbuf.at[slot], ps.at[slot], pr.at[slot], partner))
+
+    def pair_sum(slot):
+        spot = pbuf.at[slot]
+        send(spot, spot, ps.at[slot], pr.at[slot], partner).wait_recv()
+        mine = grads[2 * chip_at(place + order[slot], chips) + core]
+        return mine.astype(jnp.float32) + pbuf[slot].astype(jnp.float32)
+
+    def arrived(spot, s_sem, r_sem):
+        send(spot, spot, s_sem, r_sem, partner).wait_recv()
+
+    first = pair_sum(0).astype(jnp.bfloat16)
+    rstage[0, :, :half] = first[:, :half]
+    go(send(rstage.at[0, :, low], rbuf.at[0, :, low], rs.at[0], rr.at[0], right))
+    lstage[0, :, half:] = first[:, half:]
+    go(send(lstage.at[0, :, high], lbuf.at[0, :, high], ls.at[0], lr.at[0], left))
+    arrived(vpart, vps.at[0], vpr.at[0])
+    vslots[chip] = vec[...] + vpart[...]
+    go(send(vslots.at[chip], vslots.at[chip], vrs.at[0], vrr.at[0], right))
+    go(send(vslots.at[chip], vslots.at[chip], vls.at[0], vlr.at[0], left))
+    for step in range(1, top):
+        for side, buf, stage, s_sem, r_sem, onward in (
+            (0, rbuf, rstage, rs, rr, right),
+            (1, lbuf, lstage, ls, lr, left),
+        ):
+            total = pair_sum(2 * step - 1 + side)
+            if step == 1:
+                cols = (low, high)[side]
+                arrived(buf.at[0, :, cols], s_sem.at[0], r_sem.at[0])
+                more = buf[0, :, side * half : (side + 1) * half].astype(jnp.float32)
+                if side == 0:
+                    stage[step, :, :half] = (total[:, :half] + more).astype(jnp.bfloat16)
+                    stage[step, :, half:] = total[:, half:].astype(jnp.bfloat16)
+                else:
+                    stage[step, :, :half] = total[:, :half].astype(jnp.bfloat16)
+                    stage[step, :, half:] = (total[:, half:] + more).astype(jnp.bfloat16)
+            else:
+                arrived(buf.at[step - 1], s_sem.at[step - 1], r_sem.at[step - 1])
+                stage[step] = (total + buf[step - 1].astype(jnp.float32)).astype(jnp.bfloat16)
+            go(send(stage.at[step], buf.at[step], s_sem.at[step], r_sem.at[step], onward))
+        spot = vslots.at[chip_at(place - step, chips)]
+        arrived(spot, vrs.at[step - 1], vrr.at[step - 1])
+        go(send(spot, spot, vrs.at[step], vrr.at[step], right))
+        spot = vslots.at[chip_at(place + step, chips)]
+        arrived(spot, vls.at[step - 1], vlr.at[step - 1])
+        if step < top - 1:
+            go(send(spot, spot, vls.at[step], vlr.at[step], left))
+    spot = vslots.at[chip_at(place - top, chips)]
+    arrived(spot, vrs.at[top - 1], vrr.at[top - 1])
+    vec_out[...] = jnp.sum(vslots[...], axis=0)
+    total = pair_sum(len(order) - 1)
+    arrived(rbuf.at[top - 1], rs.at[top - 1], rr.at[top - 1])
+    arrived(lbuf.at[top - 1], ls.at[top - 1], lr.at[top - 1])
+    out[...] = total + rbuf[top - 1].astype(jnp.float32) + lbuf[top - 1].astype(jnp.float32)
+    for copy in started:
+        copy.wait_send()
+
+
+def scatter_rows(grads, vectors):
+    count = lax.axis_size("dp")
+    chips = count // 2
+    top = chips // 2
+    rows, width = grads.shape[0] // count, grads.shape[1]
+    lines = vectors.shape[0] // 128
+    dma, vmem = pltpu.SemaphoreType.DMA, pl.BlockSpec(memory_space=pltpu.VMEM)
+    block = (rows, width)
+    shard, sums = pl.pallas_call(
+        lambda *refs: scatter_kernel(chips, *refs),
+        out_shape=(
+            jax.ShapeDtypeStruct(block, jnp.float32),
+            jax.ShapeDtypeStruct((lines, 128), jnp.float32),
+        ),
+        in_specs=[vmem, vmem],
+        out_specs=(vmem, vmem),
+        scratch_shapes=[pltpu.VMEM((chips, *block), jnp.bfloat16)]
+        + [pltpu.VMEM((top, *block), jnp.bfloat16)] * 4
+        + [pltpu.VMEM((lines, 128), jnp.float32), pltpu.VMEM((chips, lines, 128), jnp.float32)]
+        + [dma((chips,))] * 2
+        + [dma((top,))] * 4
+        + [dma((1,))] * 2
+        + [dma((top,))] * 4,
+        compiler_params=pltpu.CompilerParams(collective_id=1, has_side_effects=True),
+        name="scatter_rows",
+    )(grads.reshape(count, rows, width), vectors.reshape(lines, 128))
+    return shard, sums.reshape(-1)
 
 
 def body(
@@ -121,8 +327,8 @@
     heads_width, hidden_width = w_out.shape[1], w_fc1.shape[1]
     attn_shards = jnp.concatenate([w_qkv[0], w_qkv[1], w_qkv[2], w_out], axis=1)
     mlp_shards = jnp.concatenate([w_fc1, w_fc2], axis=1)
-    attn_full = lax.all_gather(attn_shards, "dp", axis=0, tiled=True)
     mlp_full = lax.all_gather(mlp_shards, "dp", axis=0, tiled=True)
+    attn_full = gather_rows(attn_shards)
     qkv_full, out_full = attn_full[:, : 3 * heads_width], attn_full[:, 3 * heads_width :]
     fc1_full, fc2_full = mlp_full[:, :hidden_width], mlp_full[:, hidden_width:]
     allowed, live_rows = seq_masks(seq_lens, tokens.shape[0])
@@ -179,7 +385,6 @@
     stacked = jnp.concatenate([d_query, d_key, d_value], axis=1)
     g_qkv = product("td,tc->dc", low1, stacked)
     g_attn = jnp.concatenate([g_qkv.astype(jnp.bfloat16), g_out.astype(jnp.bfloat16)], axis=1)
-    shard_attn = lax.psum_scatter(g_attn, "dp", scatter_dimension=0, tiled=True)
     g_bqv = jnp.stack(
         [jnp.sum(d_query.astype(jnp.float32), axis=0), jnp.sum(d_value.astype(jnp.float32), axis=0)]
     )
@@ -190,9 +395,7 @@
     input_gradient = hidden_first_gradient + layer_norm_backward(
         first_norm_delta, layer_norm_gain[0], first_centered_scaled, first_inverse_deviation
     )
-    shard_attn, shard_mlp = shard_attn.astype(jnp.float32), shard_mlp.astype(jnp.float32)
-    shard_qkv = jnp.stack([shard_attn[:, i * heads_width : (i + 1) * heads_width] for i in range(3)])
-    shard_out = shard_attn[:, 3 * heads_width :]
+    shard_mlp = shard_mlp.astype(jnp.float32)
     shard_fc1, shard_fc2 = shard_mlp[:, :hidden_width], shard_mlp[:, hidden_width:]
     vectors = jnp.concatenate(
         [
@@ -206,7 +409,9 @@
             g_bfc2,
         ]
     )
-    vectors = sum_dp(vectors)
+    shard_attn, vectors = scatter_rows(g_attn, vectors)
+    shard_qkv = jnp.stack([shard_attn[:, i * heads_width : (i + 1) * heads_width] for i in range(3)])
+    shard_out = shard_attn[:, 3 * heads_width :]
     width = tokens.shape[1]
     cuts = [2 * width, 4 * width, 4 * width + 2 * heads_width]
     cuts += [cuts[-1] + width, cuts[-1] + width + hidden_width]

time: 375 us -> 251 us (0.67)
  waiting for transfers between devices: 227 us -> 55.9 us
  Pallas kernels: 0 us -> 99.2 us
  blocking collectives: 58.6 us -> 0 us
  matrix products: 31.9 us -> 39.5 us
    pallas_call x0 -> x2, Pallas kernels: none -> 99.2 us  [the longest x1 51.3 us: scatter_rows(): pl.pallas_call(lambda *refs: scatter_kernel(chips, *refs), out_shape=(jax...]
    reduce_scatter x1, waiting for transfers between devices: 77.4 us -> 0.01 us  [body(): shard_mlp = lax.psum_scatter(g_mlp, 'dp', scatter_dimension=0, tiled=True)]
    psum x1 -> x0, blocking collectives: 58.6 us -> none  [sum_dp(): return lax.psum(vectors, 'dp')]
    all_gather x1 -> x0, waiting for transfers between devices: 51.2 us -> none  [body(): attn_full = lax.all_gather(attn_shards, 'dp', axis=0, tiled=True)]
    all_gather x1, waiting for transfers between devices: 54.1 us -> 18.4 us  [body(): mlp_full = lax.all_gather(mlp_shards, 'dp', axis=0, tiled=True)]
    dot_general x15, matrix products: 23.6 us -> 31.8 us  [product(): return jnp.einsum(spec, left, right, preferred_element_type=jnp.float32)]
    ppermute x4, waiting for transfers between devices: 44.1 us -> 37.5 us  [sum_tensor(): other = lax.ppermute(low, 'tensor', [(0, 1), (1, 0)])]
  transfers between devices with their start and end apart: 8 -> 6, of which waited for: 7 -> 5; matrix products, arithmetic and copies ran while one was open for 11% -> 19% of each run, Pallas kernels for 0% -> 40%
where the time goes in v2:
time: 251 us; the launch traced here: 250 us
  Pallas kernels  99.2 us (40%)
  waiting for transfers between devices  55.9 us (22%)
  matrix products  39.5 us (16%)
  other arithmetic  21.4 us (9%)
  between operations  14.7 us (6%)
  local copies, waits for them, and re-layouts  14 us (6%)
  starting transfers between devices  5.19 us (2%)
    pallas_call x1, Pallas kernels, scatter_rows(): pl.pallas_call(lambda *refs: scatter_kernel(chips, *refs), out_shape=(jax...  51.3 us
    pallas_call x1, Pallas kernels, gather_rows(): pl.pallas_call(lambda *refs: gather_kernel(chips, *refs), out_shape=jax.S...  47.9 us
    ppermute x4, waiting for transfers between devices, sum_tensor(): other = lax.ppermute(low, 'tensor', [(0, 1), (1, 0)])  37.5 us
    dot_general x15, matrix products, product(): return jnp.einsum(spec, left, right, preferred_element_type=jnp.float32)  31.8 us
    all_gather x1, waiting for transfers between devices, body(): mlp_full = lax.all_gather(mlp_shards, 'dp', axis=0, tiled=True)  18.4 us
    concatenate x1, other arithmetic, body(): jnp.concatenate([g_fc1.astype(jnp.bfloat16), g_fc2.astype(jnp.bfloat16)],...  7.8 us
    ppermute x4, starting transfers between devices, sum_tensor(): other = lax.ppermute(low, 'tensor', [(0, 1), (1, 0)])  5.11 us
  transfers between devices with their start and end apart: 6, of which 5 were waited for; matrix products, arithmetic and copies ran while one was open for 19% of the time, Pallas kernels for 40%

profile of v2, /device:TPU:0, one launch (start us, length us, event | category | flops | bytes accessed | tf_op | source)
XLA Modules:
  0.0 249.8 jit_solution(9931296457028700911)
XLA Ops:
  7.2 1.9 pad_maximum_fusion.3
  9.2 0.9 slice_bitcast_fusion.5
  10.1 1.6 pad_maximum_fusion.7.refs_0_
  11.6 47.9 %gather_rows.1 = bf16[16,64,2048]{2,1,0:T(8,128)(2,1)} custom-call(bf16[64,2048]{1,0:T(8,128)(2,1)} %pad_maximum_fusion.7.refs_0_), custom_call_target="tpu_custom_call" | custom-call | tf_op jit(solution)/shard_map/gather_rows/pallas_call | solution.py:187
  59.6 0.1 convert_reduce_fusion.1
  59.8 0.3 fusion.49
  60.1 3.8 %fusion.10 = f32[256,1536]{1,0:T(8,128)S(1)} fusion(bf16[1024,2048]{1,0:T(8,128)(2,1)} %bitcast.69, bf16[256,1024]{1,0:T(8,128)(2,1)S(1)} %copy-done.2, f32[1024]{0:T(1024)S(1)} %bitcast.104, f32[1024]{0:T(1024)S(1)} %bitcast.96, f32[256]{0:T(256)S(1)} %add_rsqrt_fusion.1, f32[256]{0:T(256)S(1)} %broadcast_multiply_fusion.5), kind=kOutput, calls=%fused_computation.17 | convolution fusion | flops 806879232 | bytes 5253120 | tf_op jit(solution)/shard_map/td,dc->tc/dot_general | solution.py:16
  64.0 0.1 fusion.59
  64.2 0.1 copy.49
  64.3 0.1 copy.50
  64.5 0.1 copy.48
  64.6 0.2 reduce-window.4
  64.9 0.1 fusion.65
  65.0 0.5 fusion.78
  65.5 0.3 exponential_reduce_fusion
  65.9 0.5 convolution_convert_fusion.9
  66.4 1.8 convolution_convert_fusion.4
  68.2 1.5 collective-permute-start
  69.7 0.6 slice.79
  70.3 0.6 iota_compare_fusion.2
  71.0 11.4 %collective-permute-done = bf16[256,1024]{1,0:T(8,128)(2,1)S(1)} collective-permute-done((bf16[256,1024]{1,0:T(8,128)(2,1)S(1)}, bf16[256,1024]{1,0:T(8,128)(2,1)S(1)}, u32[]{:S(2)}, u32[]{:S(2)}) %collective-permute-start) | collective-permute-done | bytes 524320 | tf_op jit(solution)/shard_map/ppermute | solution.py:100
  82.4 0.3 fusion.71
  82.7 0.3 multiply_reduce_fusion.2
  83.0 18.4 %all-gather.2.cloned.1.call-done = bf16[1024,4096]{1,0:T(8,128)(2,1)} async-done(((bf16[64,4096]{1,0:T(8,128)(2,1)}), bf16[1024,4096]{1,0:T(8,128)(2,1)}) %all-gather.2.cloned.1.call-update) | async-done | bytes 8388624 | tf_op jit(solution)/shard_map/all_gather | solution.py:330
  101.4 3.7 %fusion.12 = f32[256,2048]{1,0:T(8,128)S(1)} fusion(bf16[1024,4096]{1,0:T(8,128)(2,1)} %all-gather.2.cloned.1.call-done, f32[2048]{0:T(1024)S(1)} %copy-done.22, f32[256,1024]{1,0:T(8,128)S(1)} %get-tuple-element.27, f32[1024]{0:T(1024)S(1)} %bitcast.93, f32[1024]{0:T(1024)S(1)} %bitcast.89, f32[256]{0:T(256)S(1)} %add_rsqrt_fusion, ...), kind=kOutput, calls=%fused_computation.19 | convolution fusion | flops 1075576832 | bytes 7358464 | tf_op jit(solution)/shard_map/dot_general | solution.py:352
  105.2 3.5 %convolution_convert_fusion.1 = bf16[1024,2048]{1,0:T(8,128)(2,1)} fusion(bf16[256,1024]{1,0:T(8,128)(2,1)S(1)} %copy-done.12, pred[256]{0:T(512)(128)(4,1)S(1)} %iota_compare_fusion.2, f32[256,2048]{1,0:T(8,128)S(1)} %fusion.12), kind=kOutput, calls=%fused_computation.3 | convolution fusion | flops 1080819712 | bytes 6816000 | tf_op jit(solution)/shard_map/td,tf->df/dot_general | solution.py:16
  108.7 0.7 slice-done.1
  109.4 2.3 convert_reduce_fusion
  111.7 1.0 copy-done.11
  112.7 3.4 %convolution_convert_fusion.2 = bf16[1024,2048]{1,0:T(8,128)(2,1)} fusion(bf16[256,2048]{1,0:T(8,128)(2,1)S(1)} %get-tuple-element.60, f32[256,1024]{1,0:T(8,128)S(1)} %get-tuple-element.27, f32[1024]{0:T(1024)S(1)} %bitcast.94, f32[1024]{0:T(1024)S(1)} %bitcast.90, f32[256]{0:T(256)S(1)} %add_rsqrt_fusion, f32[256]{0:T(256)S(1)} %broadcast_multiply_fusion.4), kind=kOutput, calls=%fused_computation.4 | convolution fusion | flops 1077149696 | bytes 6301696 | tf_op jit(solution)/shard_map/td,tf->df/dot_general | solution.py:16
  116.1 7.8 %pad_maximum_fusion = bf16[1024,4096]{1,0:T(8,128)(2,1)} fusion(bf16[1024,2048]{1,0:T(8,128)(2,1)} %convolution_convert_fusion.1, bf16[1024,2048]{1,0:T(8,128)(2,1)} %convolution_convert_fusion.2), kind=kLoop, calls=%fused_computation | loop fusion | flops 16777216 | bytes 16777216 | tf_op jit(solution)/shard_map/concatenate | solution.py:368
  123.9 4.1 %fusion.30 = bf16[256,1024]{1,0:T(8,128)(2,1)S(1)} fusion(bf16[256,2048]{1,0:T(8,128)(2,1)} %copy-done.11, bf16[1024,4096]{1,0:T(8,128)(2,1)} %all-gather.2.cloned.1.call-done), kind=kOutput, calls=%fused_computation.42 | convolution fusion | flops 1074003968 | bytes 5767168 | tf_op jit(solution)/shard_map/tf,df->td/dot_general | solution.py:16
  128.1 1.5 collective-permute-start.2
  129.6 4.1 %fusion.33 = bf16[256,1024]{1,0:T(8,128)(2,1)S(1)} fusion(bf16[1024,4096]{1,0:T(8,128)(2,1)} %all-gather.2.cloned.1.call-done, f32[256,2048]{1,0:T(8,128)S(1)} %copy-done.25), kind=kOutput, calls=%fused_computation.43 | convolution fusion | flops 1078722560 | bytes 6815744 | tf_op jit(solution)/shard_map/tf,df->td/dot_general | solution.py:16
  133.7 0.6 collective-permute-start.1
  134.3 8.7 %collective-permute-done.2 = bf16[256,1024]{1,0:T(8,128)(2,1)S(1)} collective-permute-done((bf16[256,1024]{1,0:T(8,128)(2,1)S(1)}, bf16[256,1024]{1,0:T(8,128)(2,1)S(1)}, u32[]{:S(2)}, u32[]{:S(2)}) %collective-permute-start.2) | collective-permute-done | bytes 524320 | tf_op jit(solution)/shard_map/ppermute | solution.py:100
  142.9 0.6 multiply_reduce_fusion
  143.5 9.9 %collective-permute-done.1 = bf16[256,1024]{1,0:T(8,128)(2,1)S(1)} collective-permute-done((bf16[256,1024]{1,0:T(8,128)(2,1)S(1)}, bf16[256,1024]{1,0:T(8,128)(2,1)S(1)}, u32[]{:S(2)}, u32[]{:S(2)}) %collective-permute-start.1) | collective-permute-done | bytes 524320 | tf_op jit(solution)/shard_map/ppermute | solution.py:100
  153.4 1.6 fusion.70
  155.0 1.0 copy-done
  156.0 1.7 convolution_convert_fusion.8
  157.7 0.1 copy.52
  157.9 1.6 multiply_convert_fusion
  159.5 1.0 convert_reduce_fusion.4
  160.6 1.2 convert_reduce_fusion.3
  161.9 1.4 convolution_convert_fusion.6
  163.3 3.2 %fusion.27 = bf16[256,1024]{1,0:T(8,128)(2,1)S(1)} fusion(bf16[1024,2048]{1,0:T(8,128)(2,1)} %bitcast.72, bf16[256,512]{0,1:T(8,128)(2,1)} %bitcast.83, bf16[256,512]{0,1:T(8,128)(2,1)S(1)} %bitcast.87, bf16[256,512]{0,1:T(8,128)(2,1)} %bitcast.85), kind=kOutput, calls=%fused_computation.40 | convolution fusion | flops 807927808 | bytes 4456448 | tf_op jit(solution)/shard_map/tc,dc->td/dot_general | solution.py:16
  166.6 1.5 collective-permute-start.3
  168.1 1.2 convolution_convert_fusion
  169.3 0.5 convolution_convert_fusion.3
  169.8 2.6 %pad_maximum_fusion.1 = bf16[1024,2048]{1,0:T(8,128)(2,1)} fusion(bf16[1024,512]{1,0:T(8,128)(2,1)S(1)} %convolution_convert_fusion.3, bf16[1024,1536]{1,0:T(8,128)(2,1)S(1)} %convolution_convert_fusion), kind=kLoop, calls=%fused_computation.1 | loop fusion | flops 8388608 | bytes 8388608 | tf_op jit(solution)/shard_map/concatenate | solution.py:387
  172.4 7.4 %collective-permute-done.3 = bf16[256,1024]{1,0:T(8,128)(2,1)S(1)} collective-permute-done((bf16[256,1024]{1,0:T(8,128)(2,1)S(1)}, bf16[256,1024]{1,0:T(8,128)(2,1)S(1)}, u32[]{:S(2)}, u32[]{:S(2)}) %collective-permute-start.3) | collective-permute-done | bytes 524320 | tf_op jit(solution)/shard_map/ppermute | solution.py:100
  179.9 0.6 fusion.48
  180.6 0.6 copy-done.16
  181.2 51.3 %scatter_rows.1 = (f32[64,2048]{1,0:T(8,128)}, f32[72,128]{1,0:T(8,128)}) custom-call(bf16[16,64,2048]{2,1,0:T(8,128)(2,1)} %bitcast.68, f32[72,128]{1,0:T(8,128)} %bitcast.95), custom_call_target="tpu_custom_call" | custom-call | tf_op jit(solution)/shard_map/scatter_rows/pallas_call | solution.py:291
  232.4 1.3 slice_bitcast_fusion.7
  233.7 0.6 reshape.208
  234.3 1.3 slice_bitcast_fusion.6
  235.7 0.6 reshape.207
  236.3 0.6 reshape.206
  236.9 1.8 fusion.74
  238.7 0.8 pad_maximum_fusion.4
  239.5 1.4 fusion.47
  240.9 2.1 fusion.73
  (84 shorter events, 0.7 us)
Async XLA Ops:
  7.2 94.2 %all-gather.2.cloned.1.call-start = ((), (), s32[]{:S(2)}) async-start(), calls=%async_computation.1 | async-start | bytes 8912896 | tf_op jit(solution)/shard_map/all_gather | solution.py:330
  9.1 231.8 %reduce-scatter.2.cloned.1.call-start = ((), (), s32[]{:S(2)}) async-start(), calls=%async_computation.2 | async-start | bytes 8912896 | tf_op jit(solution)/shard_map/reduce_scatter | solution.py:369
  11.6 48.0 %copy-start.2 = (bf16[256,1024]{1,0:T(8,128)(2,1)S(1)}, bf16[256,1024]{1,0:T(8,128)(2,1)}, u32[]{:S(2)}) copy-start(bf16[256,1024]{1,0:T(8,128)(2,1)} %param.13) | copy-start | bytes 1572868
  11.6 48.4 %copy-start.17 = (f32[2,1024]{1,0:T(2,128)S(1)}, f32[2,1024]{1,0:T(2,128)}, u32[]{:S(2)}) copy-start(f32[2,1024]{1,0:T(2,128)} %param.16) | copy-start | bytes 24580
  11.6 48.4 %copy-start.18 = (f32[2,1024]{1,0:T(2,128)S(1)}, f32[2,1024]{1,0:T(2,128)}, u32[]{:S(2)}) copy-start(f32[2,1024]{1,0:T(2,128)} %param.17) | copy-start | bytes 24580
  60.1 3.9 %copy-start.21 = (f32[2,512]{1,0:T(2,128)S(1)}, f32[2,512]{1,0:T(2,128)}, u32[]{:S(2)}) copy-start(f32[2,512]{1,0:T(2,128)} %param.19) | copy-start | bytes 12292
  63.9 0.7 copy-start.23
  64.3 1.5 copy-start.8
  64.4 1.4 copy-start.9
  64.6 1.3 copy-start.5
  65.9 16.5 %copy-start.3 = (bf16[256,1024]{1,0:T(8,128)(2,1)S(1)}, bf16[256,1024]{1,0:T(8,128)(2,1)}, u32[]{:S(2)}) copy-start(bf16[256,1024]{1,0:T(8,128)(2,1)} %param.13) | copy-start | bytes 1572868
  65.9 16.5 %copy-start.19 = (f32[1024]{0:T(1024)S(1)}, f32[1024]{0:T(1024)}, u32[]{:S(2)}) copy-start(f32[1024]{0:T(1024)} %param.21) | copy-start | bytes 12292
  66.4 91.5 %copy-start.6 = (bf16[8,64,256]{2,1,0:T(8,128)(2,1)}, bf16[8,64,256]{2,1,0:T(8,128)(2,1)S(1)}, u32[]{:S(2)}) copy-start(bf16[8,64,256]{2,1,0:T(8,128)(2,1)S(1)} %convolution_convert_fusion.9) | copy-start | bytes 786436
  68.2 33.2 %copy-start.22 = (f32[2048]{0:T(1024)S(1)}, f32[2048]{0:T(1024)}, u32[]{:S(2)}) copy-start(f32[2048]{0:T(1024)} %param.23) | copy-start | bytes 24580
  68.2 14.2 %collective-permute-start = (bf16[256,1024]{1,0:T(8,128)(2,1)S(1)}, bf16[256,1024]{1,0:T(8,128)(2,1)S(1)}, u32[]{:S(2)}, u32[]{:S(2)}) collective-permute-start(bf16[256,1024]{1,0:T(8,128)(2,1)S(1)} %convolution_convert_fusion.4), channel_id=1, source_target_pairs={{0,1},{1,0},{2,3},{3,2},{4,5},{5,4},{6,7},{7,6},{8,9},{9,8},{10,11... | collective-permute-start | bytes 1572872 | tf_op jit(solution)/shard_map/ppermute | solution.py:100
  101.4 3.7 %copy-start.12 = (bf16[256,1024]{1,0:T(8,128)(2,1)S(1)}, bf16[256,1024]{1,0:T(8,128)(2,1)}, u32[]{:S(2)}) copy-start(bf16[256,1024]{1,0:T(8,128)(2,1)} %param.14) | copy-start | bytes 1572868
  101.4 7.2 %slice-start = ((s8[8388608]{0:T(1024)(128)(4,1)}), s8[4194304]{0:T(1024)(128)(4,1)S(1)}, s32[]{:S(2)}) async-start(s8[8388608]{0:T(1024)(128)(4,1)} %bitcast.106), calls=%async_computation.3 | async-start | bytes 8388608
  105.1 3.5 %copy-start.24 = (f32[256,2048]{1,0:T(8,128)}, f32[256,2048]{1,0:T(8,128)S(1)}, u32[]{:S(2)}) copy-start(f32[256,2048]{1,0:T(8,128)S(1)} %fusion.12) | copy-start | bytes 6291460
  105.1 4.3 %slice-start.1 = ((s8[8388608]{0:T(1024)(128)(4,1)}), s8[4194304]{0:T(1024)(128)(4,1)S(1)}, s32[]{:S(2)}) async-start(s8[8388608]{0:T(1024)(128)(4,1)} %bitcast.106), calls=%async_computation.4 | async-start | bytes 8388608
  111.7 1.0 copy-start.11
  123.9 5.7 %copy-start.25 = (f32[256,2048]{1,0:T(8,128)S(1)}, f32[256,2048]{1,0:T(8,128)}, u32[]{:S(2)}) copy-start(f32[256,2048]{1,0:T(8,128)} %copy-done.24) | copy-start | bytes 6291460
  128.1 14.9 %collective-permute-start.2 = (bf16[256,1024]{1,0:T(8,128)(2,1)S(1)}, bf16[256,1024]{1,0:T(8,128)(2,1)S(1)}, u32[]{:S(2)}, u32[]{:S(2)}) collective-permute-start(bf16[256,1024]{1,0:T(8,128)(2,1)S(1)} %fusion.30), channel_id=1, source_target_pairs={{0,1},{1,0},{2,3},{3,2},{4,5},{5,4},{6,7},{7,6},{8,9},{9,8},{10,11... | collective-permute-start | bytes 1572872 | tf_op jit(solution)/shard_map/ppermute | solution.py:100
  133.7 19.8 %copy-start.13 = (bf16[256,1024]{1,0:T(8,128)(2,1)S(1)}, bf16[256,1024]{1,0:T(8,128)(2,1)}, u32[]{:S(2)}) copy-start(bf16[256,1024]{1,0:T(8,128)(2,1)} %param.14) | copy-start | bytes 1572868
  133.7 19.7 %copy-start.20 = (f32[1024]{0:T(1024)S(1)}, f32[1024]{0:T(1024)}, u32[]{:S(2)}) copy-start(f32[1024]{0:T(1024)} %param.25) | copy-start | bytes 12292
  133.7 19.7 %collective-permute-start.1 = (bf16[256,1024]{1,0:T(8,128)(2,1)S(1)}, bf16[256,1024]{1,0:T(8,128)(2,1)S(1)}, u32[]{:S(2)}, u32[]{:S(2)}) collective-permute-start(bf16[256,1024]{1,0:T(8,128)(2,1)S(1)} %fusion.33), channel_id=1, source_target_pairs={{0,1},{1,0},{2,3},{3,2},{4,5},{5,4},{6,7},{7,6},{8,9},{9,8},{10,11... | collective-permute-start | bytes 1572872 | tf_op jit(solution)/shard_map/ppermute | solution.py:100
  155.0 1.0 copy-start
  157.8 1.7 copy-start.10
  163.3 4.8 %copy-start.4 = (bf16[256,1024]{1,0:T(8,128)(2,1)S(1)}, bf16[256,1024]{1,0:T(8,128)(2,1)}, u32[]{:S(2)}) copy-start(bf16[256,1024]{1,0:T(8,128)(2,1)} %param.13) | copy-start | bytes 1572868
  163.3 4.8 %copy-start.14 = (bf16[8,64,256]{2,1,0:T(8,128)(2,1)S(1)}, bf16[8,64,256]{2,1,0:T(8,128)(2,1)}, u32[]{:S(2)}) copy-start(bf16[8,64,256]{2,1,0:T(8,128)(2,1)} %get-tuple-element.56) | copy-start | bytes 786436
  163.3 4.8 %copy-start.15 = (bf16[8,64,256]{2,1,0:T(8,128)(2,1)S(1)}, bf16[8,64,256]{2,1,0:T(8,128)(2,1)}, u32[]{:S(2)}) copy-start(bf16[8,64,256]{2,1,0:T(8,128)(2,1)} %get-tuple-element.58) | copy-start | bytes 786436
  166.5 2.8 %copy-start.1 = (f32[256,1024]{1,0:T(8,128)S(1)}, f32[256,1024]{1,0:T(8,128)}, u32[]{:S(2)}) copy-start(f32[256,1024]{1,0:T(8,128)} %copy-done) | copy-start | bytes 3145732
  166.5 2.8 %copy-start.7 = (bf16[8,64,256]{2,1,0:T(8,128)(2,1)S(1)}, bf16[8,64,256]{2,1,0:T(8,128)(2,1)}, u32[]{:S(2)}) copy-start(bf16[8,64,256]{2,1,0:T(8,128)(2,1)} %copy-done.6) | copy-start | bytes 786436
  166.6 13.3 %collective-permute-start.3 = (bf16[256,1024]{1,0:T(8,128)(2,1)S(1)}, bf16[256,1024]{1,0:T(8,128)(2,1)S(1)}, u32[]{:S(2)}, u32[]{:S(2)}) collective-permute-start(bf16[256,1024]{1,0:T(8,128)(2,1)S(1)} %fusion.27), channel_id=1, source_target_pairs={{0,1},{1,0},{2,3},{3,2},{4,5},{5,4},{6,7},{7,6},{8,9},{9,8},{10,11... | collective-permute-start | bytes 1572872 | tf_op jit(solution)/shard_map/ppermute | solution.py:100
  180.5 0.6 copy-start.16
Sparse Core Ops, SparseCore 0:
  10.7 90.6 all-gather.1
  124.0 114.9 reduce-scatter.1

commit v3 on v2

--- a/solution.py
+++ b/solution.py
@@ -197,7 +197,7 @@
 
 
 def scatter_kernel(
-    chips, grads, vec, out, vec_out,
+    chips, parts, vec, out, vec_out,
     pbuf, rbuf, lbuf, rstage, lstage, vpart, vslots,
     ps, pr, rs, rr, ls, lr, vps, vpr, vrs, vrr, vls, vlr,
 ):
@@ -220,14 +220,22 @@
         order += [top - step, step - top]
     order.append(0)
     go(send(vec, vpart, vps.at[0], vpr.at[0], partner))
+    spans, edge = [], 0
+    for part in parts:
+        spans.append(pl.ds(edge, part.shape[2]))
+        edge += part.shape[2]
     for slot, step in enumerate(order):
-        mine = grads.at[2 * chip_at(place + step, chips) + 1 - core]
-        go(send(mine, pbuf.at[slot], ps.at[slot], pr.at[slot], partner))
+        theirs = 2 * chip_at(place + step, chips) + 1 - core
+        for i, (part, span) in enumerate(zip(parts, spans)):
+            spot = pbuf.at[slot, :, span]
+            go(send(part.at[theirs], spot, ps.at[i, slot], pr.at[i, slot], partner))
 
     def pair_sum(slot):
-        spot = pbuf.at[slot]
-        send(spot, spot, ps.at[slot], pr.at[slot], partner).wait_recv()
-        mine = grads[2 * chip_at(place + order[slot], chips) + core]
+        for i, span in enumerate(spans):
+            spot = pbuf.at[slot, :, span]
+            send(spot, spot, ps.at[i, slot], pr.at[i, slot], partner).wait_recv()
+        ours = 2 * chip_at(place + order[slot], chips) + core
+        mine = jnp.concatenate([part[ours] for part in parts], axis=1)
         return mine.astype(jnp.float32) + pbuf[slot].astype(jnp.float32)
 
     def arrived(spot, s_sem, r_sem):
@@ -284,28 +292,29 @@
     count = lax.axis_size("dp")
     chips = count // 2
     top = chips // 2
-    rows, width = grads.shape[0] // count, grads.shape[1]
+    rows, width = grads[0].shape[0] // count, sum(part.shape[1] for part in grads)
+    amount = len(grads)
     lines = vectors.shape[0] // 128
     dma, vmem = pltpu.SemaphoreType.DMA, pl.BlockSpec(memory_space=pltpu.VMEM)
     block = (rows, width)
     shard, sums = pl.pallas_call(
-        lambda *refs: scatter_kernel(chips, *refs),
+        lambda *refs: scatter_kernel(chips, refs[:amount], *refs[amount:]),
         out_shape=(
             jax.ShapeDtypeStruct(block, jnp.float32),
             jax.ShapeDtypeStruct((lines, 128), jnp.float32),
         ),
-        in_specs=[vmem, vmem],
+        in_specs=[vmem] * (amount + 1),
         out_specs=(vmem, vmem),
         scratch_shapes=[pltpu.VMEM((chips, *block), jnp.bfloat16)]
         + [pltpu.VMEM((top, *block), jnp.bfloat16)] * 4
         + [pltpu.VMEM((lines, 128), jnp.float32), pltpu.VMEM((chips, lines, 128), jnp.float32)]
-        + [dma((chips,))] * 2
+        + [dma((amount, chips))] * 2
         + [dma((top,))] * 4
         + [dma((1,))] * 2
         + [dma((top,))] * 4,
         compiler_params=pltpu.CompilerParams(collective_id=1, has_side_effects=True),
         name="scatter_rows",
-    )(grads.reshape(count, rows, width), vectors.reshape(lines, 128))
+    )(*[part.reshape(count, rows, -1) for part in grads], vectors.reshape(lines, 128))
     return shard, sums.reshape(-1)
 
 
@@ -353,9 +362,6 @@
     act, slope = gelu_parts(pre_act)
     act_low = act.astype(jnp.bfloat16)
     mlp_part = product("tf,df->td", act_low, fc2_full)
-    mlp_mix = sum_tensor(mlp_part)
-    result = first_hidden_state + mlp_mix + b_fc2
-    output = jnp.where(live_rows[:, None], result, 0.0).astype(jnp.bfloat16)
     qkv_back, out_back, fc1_back, fc2_back = (qkv_full, out_full, fc1_full, fc2_full)
     grad_y = jnp.where(live_rows[:, None], cotangent, jnp.zeros_like(cotangent))
     flat_output_gradient = grad_y.astype(jnp.float32)
@@ -365,11 +371,14 @@
     g_fc2 = product("td,tf->df", grad_y, act_low)
     g_bfc2 = jnp.sum(flat_output_gradient, axis=0)
     g_fc1 = product("td,tf->df", low2, d_pre)
-    g_mlp = jnp.concatenate([g_fc1.astype(jnp.bfloat16), g_fc2.astype(jnp.bfloat16)], axis=1)
-    shard_mlp = lax.psum_scatter(g_mlp, "dp", scatter_dimension=0, tiled=True)
+    g_fc2 = g_fc2.astype(jnp.bfloat16)
+    shard_fc2 = lax.psum_scatter(g_fc2, "dp", scatter_dimension=0, tiled=True)
     g_bfc1 = jnp.sum(d_pre.astype(jnp.float32), axis=0)
     d_norm2_part = product("tf,df->td", d_pre, fc1_back)
-    second_norm_delta = sum_tensor(d_norm2_part)
+    mlp_low, second_norm_delta = lax.optimization_barrier(
+        (mlp_part.astype(jnp.bfloat16), sum_tensor(d_norm2_part))
+    )
+    mlp_mix = sum_tensor(mlp_low)
     second_gain_gradient = jnp.sum(second_norm_delta * second_centered_scaled, axis=0)
     g_shift2 = jnp.sum(second_norm_delta, axis=0)
     hidden_first_gradient = flat_output_gradient + layer_norm_backward(
@@ -382,9 +391,12 @@
     d_query, d_key, d_value = attend_back(
         query, key_rows, value, heads_out, d_heads, logsum, allowed
     )
+    mlp_mix, d_query = lax.optimization_barrier((mlp_mix, d_query))
+    result = first_hidden_state + mlp_mix + b_fc2
+    output = jnp.where(live_rows[:, None], result, 0.0).astype(jnp.bfloat16)
     stacked = jnp.concatenate([d_query, d_key, d_value], axis=1)
     g_qkv = product("td,tc->dc", low1, stacked)
-    g_attn = jnp.concatenate([g_qkv.astype(jnp.bfloat16), g_out.astype(jnp.bfloat16)], axis=1)
+    ring_grads = [part.astype(jnp.bfloat16) for part in (g_qkv, g_out, g_fc1)]
     g_bqv = jnp.stack(
         [jnp.sum(d_query.astype(jnp.float32), axis=0), jnp.sum(d_value.astype(jnp.float32), axis=0)]
     )
@@ -395,8 +407,7 @@
     input_gradient = hidden_first_gradient + layer_norm_backward(
         first_norm_delta, layer_norm_gain[0], first_centered_scaled, first_inverse_deviation
     )
-    shard_mlp = shard_mlp.astype(jnp.float32)
-    shard_fc1, shard_fc2 = shard_mlp[:, :hidden_width], shard_mlp[:, hidden_width:]
+    shard_fc2 = shard_fc2.astype(jnp.float32)
     vectors = jnp.concatenate(
         [
             first_gain_gradient,
@@ -409,9 +420,10 @@
             g_bfc2,
         ]
     )
-    shard_attn, vectors = scatter_rows(g_attn, vectors)
-    shard_qkv = jnp.stack([shard_attn[:, i * heads_width : (i + 1) * heads_width] for i in range(3)])
-    shard_out = shard_attn[:, 3 * heads_width :]
+    shard_ring, vectors = scatter_rows(ring_grads, vectors)
+    shard_qkv = jnp.stack([shard_ring[:, i * heads_width : (i + 1) * heads_width] for i in range(3)])
+    shard_out = shard_ring[:, 3 * heads_width : 4 * heads_width]
+    shard_fc1 = shard_ring[:, 4 * heads_width :]
     width = tokens.shape[1]
     cuts = [2 * width, 4 * width, 4 * width + 2 * heads_width]
     cuts += [cuts[-1] + width, cuts[-1] + width + hidden_width]

time: 251 us -> 258 us (1.028)
  Pallas kernels: 99.2 us -> 111 us
  other arithmetic: 21.4 us -> 15.4 us
  waiting for transfers between devices: 55.9 us -> 51.2 us
  matrix products: 39.5 us -> 43.3 us
    pallas_call x1, Pallas kernels: 51.3 us -> 63.1 us  [scatter_rows(): pl.pallas_call(lambda *refs: scatter_kernel(chips, refs[:amount], *refs[a...]
    concatenate x2 -> x0, other arithmetic: 10.4 us -> none  [the longest x1 7.8 us: body(): jnp.concatenate([g_fc1.astype(jnp.bfloat16), g_fc2.astype(jnp.bfloat16)],...]
    ppermute x4, waiting for transfers between devices: 37.5 us -> 32.7 us  [sum_tensor(): other = lax.ppermute(low, 'tensor', [(0, 1), (1, 0)])]
    dot_general x1, matrix products: 2.27 us -> 5.28 us  [body(): jnp.dot(grad_y, fc2_back, preferred_element_type=jnp.float32) * slope]
    convert_element_type x0 -> x2, other arithmetic: none -> 2.78 us  [the longest x1 1.78 us: body(): shard_fc2 = shard_fc2.astype(jnp.float32)]
  transfers between devices with their start and end apart: 6 -> 6, of which waited for: 5 -> 5; matrix products, arithmetic and copies ran while one was open for 19% -> 18% of each run, Pallas kernels for 40% -> 43%
where the time goes in v3:
time: 258 us; the launch traced here: 257 us
  Pallas kernels  111 us (43%)
  waiting for transfers between devices  51.2 us (20%)
  matrix products  43.3 us (17%)
  local copies, waits for them, and re-layouts  15.6 us (6%)
  other arithmetic  15.4 us (6%)
  between operations  14.6 us (6%)
  starting transfers between devices  6.1 us (2%)
    pallas_call x1, Pallas kernels, scatter_rows(): pl.pallas_call(lambda *refs: scatter_kernel(chips, refs[:amount], *refs[a...  63.1 us
    pallas_call x1, Pallas kernels, gather_rows(): pl.pallas_call(lambda *refs: gather_kernel(chips, *refs), out_shape=jax.S...  47.9 us
    ppermute x4, waiting for transfers between devices, sum_tensor(): other = lax.ppermute(low, 'tensor', [(0, 1), (1, 0)])  32.7 us
    dot_general x15, matrix products, product(): return jnp.einsum(spec, left, right, preferred_element_type=jnp.float32)  32 us
    all_gather x1, waiting for transfers between devices, body(): mlp_full = lax.all_gather(mlp_shards, 'dp', axis=0, tiled=True)  18.4 us
    ppermute x4, starting transfers between devices, sum_tensor(): other = lax.ppermute(low, 'tensor', [(0, 1), (1, 0)])  6.02 us
    dot_general x1, matrix products, body(): jnp.dot(grad_y, fc2_back, preferred_element_type=jnp.float32) * slope  5.28 us
  transfers between devices with their start and end apart: 6, of which 5 were waited for; matrix products, arithmetic and copies ran while one was open for 18% of the time, Pallas kernels for 43%

profile of v3, /device:TPU:0, one launch (start us, length us, event | category | flops | bytes accessed | tf_op | source)
XLA Modules:
  0.0 257.3 jit_solution(5215649799430204434)
XLA Ops:
  7.2 1.9 pad_maximum_fusion.1
  9.2 0.9 slice_bitcast_fusion.5
  10.1 1.6 pad_maximum_fusion.5.refs_0_
  11.6 47.9 %gather_rows.1 = bf16[16,64,2048]{2,1,0:T(8,128)(2,1)} custom-call(bf16[64,2048]{1,0:T(8,128)(2,1)} %pad_maximum_fusion.5.refs_0_), custom_call_target="tpu_custom_call" | custom-call | tf_op jit(solution)/shard_map/gather_rows/pallas_call | solution.py:187
  59.6 0.1 convert_reduce_fusion.1
  59.8 0.3 fusion.49
  60.1 3.8 %fusion.10 = f32[256,1536]{1,0:T(8,128)S(1)} fusion(bf16[1024,2048]{1,0:T(8,128)(2,1)} %bitcast.71, bf16[256,1024]{1,0:T(8,128)(2,1)S(1)} %copy-done.2, f32[1024]{0:T(1024)S(1)} %bitcast.110, f32[1024]{0:T(1024)S(1)} %bitcast.101, f32[256]{0:T(256)S(1)} %add_rsqrt_fusion.1, f32[256]{0:T(256)S(1)} %broadcast_multiply_fusion.5), kind=kOutput, calls=%fused_computation.15 | convolution fusion | flops 806879232 | bytes 5253120 | tf_op jit(solution)/shard_map/td,dc->tc/dot_general | solution.py:16
  64.6 0.2 reduce-window.4
  65.0 0.5 fusion.74
  65.5 0.3 exponential_reduce_fusion
  65.9 0.4 convolution_convert_fusion.9
  66.3 1.8 convolution_convert_fusion.4
  68.2 1.6 collective-permute-start
  69.7 0.6 slice.76
  70.3 0.6 iota_compare_fusion.2
  71.0 11.4 %collective-permute-done = bf16[256,1024]{1,0:T(8,128)(2,1)S(1)} collective-permute-done((bf16[256,1024]{1,0:T(8,128)(2,1)S(1)}, bf16[256,1024]{1,0:T(8,128)(2,1)S(1)}, u32[]{:S(2)}, u32[]{:S(2)}) %collective-permute-start) | collective-permute-done | bytes 524320 | tf_op jit(solution)/shard_map/ppermute | solution.py:100
  82.4 0.3 fusion.68
  82.7 0.3 multiply_reduce_fusion.2
  83.0 18.4 %all-gather.2.cloned.1.call-done = bf16[1024,4096]{1,0:T(8,128)(2,1)} async-done(((bf16[64,4096]{1,0:T(8,128)(2,1)}), bf16[1024,4096]{1,0:T(8,128)(2,1)}) %all-gather.2.cloned.1.call-update) | async-done | bytes 8388624 | tf_op jit(solution)/shard_map/all_gather | solution.py:339
  101.4 3.6 %fusion.12 = f32[256,2048]{1,0:T(8,128)S(1)} fusion(bf16[1024,4096]{1,0:T(8,128)(2,1)} %all-gather.2.cloned.1.call-done, f32[2048]{0:T(1024)S(1)} %copy-done.25, f32[256,1024]{1,0:T(8,128)S(1)} %get-tuple-element.35, f32[1024]{0:T(1024)S(1)} %bitcast.98, f32[1024]{0:T(1024)S(1)} %bitcast.94, f32[256]{0:T(256)S(1)} %add_rsqrt_fusion, ...), kind=kOutput, calls=%fused_computation.17 | convolution fusion | flops 1075576832 | bytes 7358464 | tf_op jit(solution)/shard_map/dot_general | solution.py:361
  105.0 1.3 copy-done.27
  106.4 3.4 %convolution_convert_fusion.1 = bf16[1024,2048]{1,0:T(8,128)(2,1)} fusion(bf16[256,1024]{1,0:T(8,128)(2,1)S(1)} %copy-done.15, pred[256]{0:T(512)(128)(4,1)S(1)} %iota_compare_fusion.2, f32[256,2048]{1,0:T(8,128)S(1)} %fusion.12), kind=kOutput, calls=%fused_computation.1 | convolution fusion | flops 1080819712 | bytes 6816000 | tf_op jit(solution)/shard_map/td,tf->df/dot_general | solution.py:16
  109.8 5.3 %convert_reduce_fusion = (f32[2048]{0:T(1024)S(1)}, bf16[256,2048]{1,0:T(8,128)(2,1)S(1)}) fusion(f32[256,2048]{1,0:T(8,128)} %copy-done.27, bf16[1024,4096]{1,0:T(8,128)(2,1)} %all-gather.2.cloned.1.call-done, bf16[256,1024]{1,0:T(8,128)(2,1)} %param.14, pred[256]{0:T(512)(128)(4,1)S(1)} %iota_compare_fusion.2), kind=kOutput, calls=%fused_computation.25 | convolution fusion | flops 1085011968 | bytes 7872768 | tf_op jit(solution)/shard_map/dot_general | solution.py:368
  115.1 3.4 %convolution_convert_fusion.2 = bf16[1024,2048]{1,0:T(8,128)(2,1)} fusion(bf16[256,2048]{1,0:T(8,128)(2,1)S(1)} %get-tuple-element.63, f32[256,1024]{1,0:T(8,128)S(1)} %get-tuple-element.35, f32[1024]{0:T(1024)S(1)} %bitcast.99, f32[1024]{0:T(1024)S(1)} %bitcast.95, f32[256]{0:T(256)S(1)} %add_rsqrt_fusion, f32[256]{0:T(256)S(1)} %broadcast_multiply_fusion.4), kind=kOutput, calls=%fused_computation.2 | convolution fusion | flops 1077149696 | bytes 6301696 | tf_op jit(solution)/shard_map/td,tf->df/dot_general | solution.py:16
  118.5 4.4 %fusion.30 = bf16[256,1024]{1,0:T(8,128)(2,1)} fusion(bf16[256,2048]{1,0:T(8,128)(2,1)S(1)} %get-tuple-element.63, bf16[1024,4096]{1,0:T(8,128)(2,1)} %all-gather.2.cloned.1.call-done), kind=kOutput, calls=%fused_computation.40 | convolution fusion | flops 1074003968 | bytes 5767168 | tf_op jit(solution)/shard_map/tf,df->td/dot_general | solution.py:16
  122.8 1.5 collective-permute-start.1
  124.3 5.3 %fusion.33 = bf16[256,1024]{1,0:T(8,128)(2,1)} fusion(bf16[1024,4096]{1,0:T(8,128)(2,1)} %all-gather.2.cloned.1.call-done, f32[256,2048]{1,0:T(8,128)} %copy-done.27), kind=kOutput, calls=%fused_computation.41 | convolution fusion | flops 1078722560 | bytes 6815744 | tf_op jit(solution)/shard_map/tf,df->td/dot_general | solution.py:16
  129.7 7.6 %collective-permute-done.1 = bf16[256,1024]{1,0:T(8,128)(2,1)} collective-permute-done((bf16[256,1024]{1,0:T(8,128)(2,1)}, bf16[256,1024]{1,0:T(8,128)(2,1)}, u32[]{:S(2)}, u32[]{:S(2)}) %collective-permute-start.1) | collective-permute-done | bytes 524320 | tf_op jit(solution)/shard_map/ppermute | solution.py:100
  137.3 1.4 convert_add_fusion.4
  138.7 0.6 multiply_reduce_fusion
  139.3 0.5 fusion.67
  139.8 1.0 copy-done
  140.8 2.4 convolution_convert_fusion.8
  143.2 1.1 copy.50
  144.3 1.2 convert_reduce_fusion.3
  145.5 1.5 collective-permute-start.2
  147.0 1.0 multiply_reduce_fusion.4
  148.1 1.6 multiply_convert_fusion
  149.7 0.4 convolution_convert_fusion.6
  150.2 0.3 convolution_convert_fusion.7
  150.5 0.4 copy-done.1
  151.0 1.5 convolution_convert_fusion.3
  152.4 6.5 %collective-permute-done.2 = bf16[256,1024]{1,0:T(8,128)(2,1)S(1)} collective-permute-done((bf16[256,1024]{1,0:T(8,128)(2,1)}, bf16[256,1024]{1,0:T(8,128)(2,1)S(1)}, u32[]{:S(2)}, u32[]{:S(2)}) %collective-permute-start.2) | collective-permute-done | bytes 524320 | tf_op jit(solution)/shard_map/ppermute | solution.py:100
  159.0 0.2 convert_add_fusion.3
  159.2 1.0 fusion.27
  160.2 0.1 convert_reduce_fusion.4
  160.4 1.5 collective-permute-start.3
  161.9 1.0 select_convert_fusion
  162.9 2.9 %convolution_convert_fusion = bf16[1024,1536]{1,0:T(8,128)(2,1)} fusion(bf16[256,512]{0,1:T(8,128)(2,1)S(1)} %bitcast.91, bf16[256,512]{0,1:T(8,128)(2,1)S(1)} %bitcast.93, bf16[256,512]{0,1:T(8,128)(2,1)S(1)} %bitcast.89, bf16[256,1024]{1,0:T(8,128)(2,1)S(1)} %copy-done.4, f32[1024]{0:T(1024)S(1)} %bitcast.111, f32[1024]{0:T(1024)S(1)} %bitcast.102, ...), kind=kOutput, calls=%fused_computation | convolution fusion | flops 810811392 | bytes 4466688 | tf_op jit(solution)/shard_map/td,tc->dc/dot_general | solution.py:16
  165.8 7.2 %collective-permute-done.3 = bf16[256,1024]{1,0:T(8,128)(2,1)S(1)} collective-permute-done((bf16[256,1024]{1,0:T(8,128)(2,1)S(1)}, bf16[256,1024]{1,0:T(8,128)(2,1)S(1)}, u32[]{:S(2)}, u32[]{:S(2)}) %collective-permute-start.3) | collective-permute-done | bytes 524320 | tf_op jit(solution)/shard_map/ppermute | solution.py:100
  173.0 0.8 copy-done.13
  173.8 0.6 fusion.48
  174.5 0.6 copy-done.19
  175.1 63.1 %scatter_rows.1 = (f32[64,4096]{1,0:T(8,128)}, f32[72,128]{1,0:T(8,128)}) custom-call(bf16[16,64,1536]{2,1,0:T(8,128)(2,1)} %bitcast.78, bf16[16,64,512]{2,1,0:T(8,128)(2,1)} %bitcast.77, bf16[16,64,2048]{2,1,0:T(8,128)(2,1)} %bitcast.70, f32[72,128]{1,0:T(8,128)} %bitcast.100), custom_call_target="tpu_custom_call" | custom-call | tf_op jit(solution)/shard_map/scatter_rows/pallas_call | solution.py:300
  238.3 1.3 slice_bitcast_fusion.7
  239.6 0.6 reshape.214
  240.2 1.3 slice_bitcast_fusion.6
  241.5 0.6 reshape.213
  242.2 0.6 reshape.212
  242.8 1.9 slice.97
  244.6 1.8 fusion.70
  246.4 0.8 pad_maximum_fusion.2
  247.2 1.4 fusion.47
  248.6 1.8 convert_element_type.178
  (85 shorter events, 1.2 us)
Async XLA Ops:
  7.2 94.2 %all-gather.2.cloned.1.call-start = ((), (), s32[]{:S(2)}) async-start(), calls=%async_computation.1 | async-start | bytes 8912896 | tf_op jit(solution)/shard_map/all_gather | solution.py:339
  9.1 239.5 %reduce-scatter.2.cloned.1.call-start = ((), (), s32[]{:S(2)}) async-start(), calls=%async_computation.2 | async-start | bytes 4456448 | tf_op jit(solution)/shard_map/reduce_scatter | solution.py:375
  11.6 48.0 %copy-start.2 = (bf16[256,1024]{1,0:T(8,128)(2,1)S(1)}, bf16[256,1024]{1,0:T(8,128)(2,1)}, u32[]{:S(2)}) copy-start(bf16[256,1024]{1,0:T(8,128)(2,1)} %param.13) | copy-start | bytes 1572868
  11.6 48.4 %copy-start.20 = (f32[2,1024]{1,0:T(2,128)S(1)}, f32[2,1024]{1,0:T(2,128)}, u32[]{:S(2)}) copy-start(f32[2,1024]{1,0:T(2,128)} %param.16) | copy-start | bytes 24580
  11.6 48.4 %copy-start.21 = (f32[2,1024]{1,0:T(2,128)S(1)}, f32[2,1024]{1,0:T(2,128)}, u32[]{:S(2)}) copy-start(f32[2,1024]{1,0:T(2,128)} %param.17) | copy-start | bytes 24580
  60.1 3.9 %copy-start.24 = (f32[2,512]{1,0:T(2,128)S(1)}, f32[2,512]{1,0:T(2,128)}, u32[]{:S(2)}) copy-start(f32[2,512]{1,0:T(2,128)} %param.19) | copy-start | bytes 12292
  63.9 0.7 copy-start.26
  64.3 1.5 copy-start.9
  64.5 1.4 copy-start.11
  64.6 1.3 copy-start.6
  65.9 16.6 %copy-start.3 = (bf16[256,1024]{1,0:T(8,128)(2,1)S(1)}, bf16[256,1024]{1,0:T(8,128)(2,1)}, u32[]{:S(2)}) copy-start(bf16[256,1024]{1,0:T(8,128)(2,1)} %param.13) | copy-start | bytes 1572868
  65.9 16.5 %copy-start.22 = (f32[1024]{0:T(1024)S(1)}, f32[1024]{0:T(1024)}, u32[]{:S(2)}) copy-start(f32[1024]{0:T(1024)} %param.21) | copy-start | bytes 12292
  66.3 4.6 %copy-start.7 = (bf16[8,64,256]{2,1,0:T(8,128)(2,1)}, bf16[8,64,256]{2,1,0:T(8,128)(2,1)S(1)}, u32[]{:S(2)}) copy-start(bf16[8,64,256]{2,1,0:T(8,128)(2,1)S(1)} %convolution_convert_fusion.9) | copy-start | bytes 786436
  68.2 33.3 %copy-start.25 = (f32[2048]{0:T(1024)S(1)}, f32[2048]{0:T(1024)}, u32[]{:S(2)}) copy-start(f32[2048]{0:T(1024)} %param.23) | copy-start | bytes 24580
  68.2 14.2 %collective-permute-start = (bf16[256,1024]{1,0:T(8,128)(2,1)S(1)}, bf16[256,1024]{1,0:T(8,128)(2,1)S(1)}, u32[]{:S(2)}, u32[]{:S(2)}) collective-permute-start(bf16[256,1024]{1,0:T(8,128)(2,1)S(1)} %convolution_convert_fusion.4), channel_id=1, source_target_pairs={{0,1},{1,0},{2,3},{3,2},{4,5},{5,4},{6,7},{7,6},{8,9},{9,8},{10,11... | collective-permute-start | bytes 1572872 | tf_op jit(solution)/shard_map/ppermute | solution.py:100
  101.4 4.9 %copy-start.15 = (bf16[256,1024]{1,0:T(8,128)(2,1)S(1)}, bf16[256,1024]{1,0:T(8,128)(2,1)}, u32[]{:S(2)}) copy-start(bf16[256,1024]{1,0:T(8,128)(2,1)} %param.14) | copy-start | bytes 1572868
  105.0 1.3 copy-start.27
  122.8 14.4 %collective-permute-start.1 = (bf16[256,1024]{1,0:T(8,128)(2,1)}, bf16[256,1024]{1,0:T(8,128)(2,1)}, u32[]{:S(2)}, u32[]{:S(2)}) collective-permute-start(bf16[256,1024]{1,0:T(8,128)(2,1)} %fusion.30), channel_id=1, source_target_pairs={{0,1},{1,0},{2,3},{3,2},{4,5},{5,4},{6,7},{7,6},{8,9},{9,8},{10,11... | collective-permute-start | bytes 1572872 | tf_op jit(solution)/shard_map/ppermute | solution.py:100
  129.7 9.6 %copy-start.16 = (bf16[256,1024]{1,0:T(8,128)(2,1)S(1)}, bf16[256,1024]{1,0:T(8,128)(2,1)}, u32[]{:S(2)}) copy-start(bf16[256,1024]{1,0:T(8,128)(2,1)} %param.14) | copy-start | bytes 1572868
  139.8 1.0 copy-start
  145.5 4.2 %copy-start.10 = (bf16[256,512]{0,1:T(8,128)(2,1)S(1)}, bf16[256,512]{0,1:T(8,128)(2,1)}, u32[]{:S(2)}) copy-start(bf16[256,512]{0,1:T(8,128)(2,1)} %copy-done.9) | copy-start | bytes 786436
  145.5 13.5 %collective-permute-start.2 = (bf16[256,1024]{1,0:T(8,128)(2,1)}, bf16[256,1024]{1,0:T(8,128)(2,1)S(1)}, u32[]{:S(2)}, u32[]{:S(2)}) collective-permute-start(bf16[256,1024]{1,0:T(8,128)(2,1)} %fusion.33), channel_id=1, source_target_pairs={{0,1},{1,0},{2,3},{3,2},{4,5},{5,4},{6,7},{7,6},{8,9},{9,8},{10,11... | collective-permute-start | bytes 1572872 | tf_op jit(solution)/shard_map/ppermute | solution.py:100
  148.0 2.1 copy-start.12
  149.7 1.2 copy-start.1
  149.7 1.3 copy-start.8
  150.2 8.8 %copy-start.17 = (bf16[256,1024]{1,0:T(8,128)(2,1)S(1)}, bf16[256,1024]{1,0:T(8,128)(2,1)}, u32[]{:S(2)}) copy-start(bf16[256,1024]{1,0:T(8,128)(2,1)} %fusion.33) | copy-start | bytes 1572868
  151.0 8.2 %copy-start.5 = (bf16[16,64,2048]{2,1,0:T(8,128)(2,1)S(1)}, bf16[16,64,2048]{2,1,0:T(8,128)(2,1)}, u32[]{:S(2)}) copy-start(bf16[16,64,2048]{2,1,0:T(8,128)(2,1)} %gather_rows.1) | copy-start | bytes 12582916
  151.0 8.2 %copy-start.18 = (bf16[8,64,256]{2,1,0:T(8,128)(2,1)S(1)}, bf16[8,64,256]{2,1,0:T(8,128)(2,1)}, u32[]{:S(2)}) copy-start(bf16[8,64,256]{2,1,0:T(8,128)(2,1)} %get-tuple-element.61) | copy-start | bytes 786436
  159.2 2.8 %copy-start.23 = (f32[1024]{0:T(1024)S(1)}, f32[1024]{0:T(1024)}, u32[]{:S(2)}) copy-start(f32[1024]{0:T(1024)} %param.25) | copy-start | bytes 12292
  160.2 2.7 %copy-start.4 = (bf16[256,1024]{1,0:T(8,128)(2,1)S(1)}, bf16[256,1024]{1,0:T(8,128)(2,1)}, u32[]{:S(2)}) copy-start(bf16[256,1024]{1,0:T(8,128)(2,1)} %param.13) | copy-start | bytes 1572868
  160.4 12.6 %collective-permute-start.3 = (bf16[256,1024]{1,0:T(8,128)(2,1)S(1)}, bf16[256,1024]{1,0:T(8,128)(2,1)S(1)}, u32[]{:S(2)}, u32[]{:S(2)}) collective-permute-start(bf16[256,1024]{1,0:T(8,128)(2,1)S(1)} %fusion.27), channel_id=1, source_target_pairs={{0,1},{1,0},{2,3},{3,2},{4,5},{5,4},{6,7},{7,6},{8,9},{9,8},{10,11... | collective-permute-start | bytes 1572872 | tf_op jit(solution)/shard_map/ppermute | solution.py:100
  173.0 0.8 copy-start.13
  174.5 0.6 copy-start.19
  238.3 9.0 %copy-start.14 = (bf16[256,1024]{1,0:T(8,128)(2,1)S(1)}, bf16[256,1024]{1,0:T(8,128)(2,1)}, u32[]{:S(2)}) copy-start(bf16[256,1024]{1,0:T(8,128)(2,1)} %copy-done.13) | copy-start | bytes 1572868
Sparse Core Ops, SparseCore 0:
  10.7 90.6 all-gather.1
  124.5 75.3 reduce-scatter.1
